TPU v7x, 32 devices: a whole 2x2x4 slice. The times are simulated.
32 devices in a mesh: groups: 2 (over x), loop: 16 (over z, y, core).
Axes of the slice: x: 2, y: 2, z: 4, core: 2. Of those that a mesh axis runs over, the one named last changes fastest.
Arguments:
- embeddings: bfloat16 [4096, 1024], P(('groups', 'loop')), parts along dimension 0
- generation: int32 [4096], P(('groups', 'loop')), parts along dimension 0, may hold values from 0 to 2047, as said below
- eligible: int32 [4096], P(('groups', 'loop')), parts along dimension 0, may hold values 0 or 1
Outputs:
- neighbour: bfloat16 [4096, 1024], P(('groups', 'loop')), parts along dimension 0
- row_max: float32 [4096], P(('groups', 'loop')), parts along dimension 0
There are 2 independent parts, one for each index of `groups`. A program takes and returns all parts, laid end to end along the dimension named above; each array names one. Nothing has to cross between parts.
Inputs may be any that keep to these rules, and one draw needn't show every extreme that they name: generation is a permutation of 0 to 2047; loop index d holds the generation indices d * 64 to d * 64 + 63 in its first 64 rows and (31 - d) * 64 to (32 - d) * 64 - 1 in its last 64 rows, in any order within each block.
All inputs are finite; a program needn't handle non-finite values. No bound on the sum of `eligible` on one device may be relied on, other than what follows from the above.
Results may differ from a plain program's by a relative error of at most 0.0035.
Values may be sent and summed in bfloat16 or wider, within the bound.
No kernel may reach another device: no remote copies, remote signals or barrier semaphores. Data moves between devices by JAX's collectives and lax.ppermute only.
A program may use at most 128 MiB of HBM per device.

v0:
```python
import functools
import math

import jax
import jax.numpy as jnp
from jax import lax
from jax.experimental import pallas as pl
from jax.experimental.pallas import tpu as pltpu
from jax.sharding import PartitionSpec as P


smoothing_divisor = 3.0
CODE_LIMIT = 4 << 20


def ring_of_chips(chips):
    across = max(k for k in range(1, int(math.isqrt(chips)) + 1) if chips % k == 0)
    down = chips // across
    order = [(0, 0)]
    for r in range(down):
        columns = range(1, across)
        order += [(r, q) for q in (columns if r % 2 == 0 else reversed(columns))]
    order += [(r, 0) for r in range(down - 1, 0, -1)]
    return [r * across + q for r, q in order]


def swaps(ring):
    size = len(ring)
    even, odd = {}, {}
    for k in range(size):
        even[ring[k]] = ring[k ^ 1]
        odd[ring[k]] = ring[(((k - 1) ^ 1) + 1) % size]
    return even, odd


def code_kernel(x_hbm, flag_hbm, gen_hbm, x_ref, early_ref, late_ref, gen_ref, flag_ref, sems):
    rows = x_ref.shape[0]
    half = rows // 2
    flag_copy = pltpu.make_async_copy(flag_hbm, flag_ref, sems.at[0])
    flag_copy.start()
    x_copy = pltpu.make_async_copy(x_hbm, x_ref, sems.at[1])
    x_copy.start()
    gen_copy = pltpu.make_async_copy(gen_hbm, gen_ref, sems.at[2])
    gen_copy.start()
    flag_copy.wait()
    row_id = lax.broadcasted_iota(jnp.int32, (rows, rows), 0)
    col_id = lax.broadcasted_iota(jnp.int32, (rows, rows), 1)
    flags = jnp.broadcast_to(flag_ref[...], (rows, rows))
    flag = jnp.sum(jnp.where(row_id == col_id, flags, 0), axis=1, keepdims=True)
    bad = (flag != 1) & (lax.broadcasted_iota(jnp.int32, (rows, 128), 1) == 0)
    x_copy.wait()
    head = jnp.where(bad, jnp.float32(jnp.nan), x_ref[:, :128].astype(jnp.float32)).astype(jnp.bfloat16)
    for k, out_ref in enumerate((early_ref, late_ref)):
        out_ref[:, :128] = head[k * half : (k + 1) * half]
        out_ref[:, 128:] = x_ref[k * half : (k + 1) * half, 128:]
    gen_copy.wait()


def later_bits(me, bits):
    word = jnp.int32(0)
    for i, b in enumerate(bits):
        word = jnp.where(me == i, jnp.int32(b), word)
    return word


def scores_into(score_ref, at, mult, x, keys_ref, word, ids, gen_ref):
    rows = x.shape[0]
    half = rows // 2
    dims = (((1,), (1,)), ((), ()))
    row_id = lax.broadcasted_iota(jnp.int32, (rows, rows), 0)
    col_id = lax.broadcasted_iota(jnp.int32, (rows, rows), 1)
    late_q, late_k = row_id >= half, col_id >= half
    keys = jnp.concatenate([r[...] for r in keys_ref], axis=0)
    s = lax.dot_general(x, keys, dims, preferred_element_type=jnp.float32) * mult
    top = None
    for k, chunk in enumerate(ids):
        t = s[:, k * rows : (k + 1) * rows]
        if chunk == 0:
            gen_k = jnp.broadcast_to(gen_ref[...], (rows, rows))
            gen_q = jnp.sum(jnp.where(row_id == col_id, gen_k, 0), axis=1, keepdims=True)
            valid = gen_k < gen_q
        else:
            later = jnp.full((rows, rows), (word >> chunk) & 1) == 1
            valid = ((~late_k) & (late_q | ~later)) | (late_q & late_k & later)
        t = jnp.where(valid & (t == t), t, -jnp.inf)
        score_ref[:, at + k * rows : at + (k + 1) * rows] = t
        top = t if top is None else jnp.maximum(top, t)
    return top


def score_kernel(mult, bits, ids, me_ref, x_ref, gen_ref, *refs):
    keys, (score_ref, top_ref) = refs[:-2], refs[-2:]
    rows = x_ref.shape[0]
    x = x_ref[...]
    word = later_bits(me_ref[0], bits)
    top = None
    for k in range(0, len(ids), 2):
        t = scores_into(score_ref, k * rows, mult, x, keys[2 * k : 2 * k + 4], word, ids[k : k + 2], gen_ref)
        top = t if top is None else jnp.maximum(top, t)
    top_ref[...] = top


def finish_kernel(mult, bits, sizes, last_ids, me_ref, x_ref, gen_ref, *refs):
    count = len(sizes)
    scores, tops, refs = refs[:count], refs[count : 2 * count], refs[2 * count :]
    keys, (out_ref, peak_ref, last_ref) = refs[:-3], refs[-3:]
    rows, _ = x_ref.shape
    x = x_ref[...]
    last_keys = keys[-2 * len(last_ids) :]
    top = scores_into(last_ref, 0, mult, x, last_keys, later_bits(me_ref[0], bits), last_ids, gen_ref)
    for t in tops:
        top = jnp.maximum(top, t[...])
    peak = jnp.maximum(jnp.max(top, axis=1, keepdims=True), 0.0)
    pieces = [(ref, j * rows) for ref, size in zip((*scores, last_ref), (*sizes, len(last_ids))) for j in range(size)]
    total = jnp.exp(-peak)
    acc = [None, None]
    edge = 2 * rows
    for k in range(0, len(pieces), 2):
        s = jnp.concatenate([ref[:, at : at + rows] for ref, at in pieces[k : k + 2]], axis=1)
        expo = jnp.exp(s - peak)
        total = total + jnp.sum(expo, axis=1, keepdims=True)
        w = expo.astype(jnp.bfloat16)
        quad = keys[2 * k : 2 * k + 4]
        head = jnp.concatenate([v[:, :edge] for v in quad], axis=0)
        head = jnp.where(head == head, head, jnp.zeros_like(head))
        tail = jnp.concatenate([v[:, edge:] for v in quad], axis=0)
        for i, v in enumerate((head, tail)):
            t = jnp.dot(w, v, preferred_element_type=jnp.float32)
            acc[i] = t if acc[i] is None else acc[i] + t
    out_ref[:, :edge] = (acc[0] / total).astype(out_ref.dtype)
    out_ref[:, edge:] = (acc[1] / total).astype(out_ref.dtype)
    row_id = lax.broadcasted_iota(jnp.int32, (rows, rows), 0)
    col_id = lax.broadcasted_iota(jnp.int32, (rows, rows), 1)
    peak_ref[...] = jnp.sum(jnp.where(row_id == col_id, peak, 0.0), axis=0, keepdims=True)


def ring_body(n, embeddings, generation, eligible):
    rows, width = embeddings.shape
    half = rows // 2
    mult = smoothing_divisor / math.sqrt(width)
    maps = swaps(ring_of_chips(n // 2))
    me = lax.axis_index("loop").reshape(1)
    vmem = pl.BlockSpec(memory_space=pltpu.VMEM)
    smem = pl.BlockSpec(memory_space=pltpu.SMEM)
    hbm = pl.BlockSpec(memory_space=pltpu.MemorySpace.HBM)
    bf16 = lambda r: jax.ShapeDtypeStruct((r, width), jnp.bfloat16)

    def swap(kind, v):
        return lax.ppermute(v, "loop", [(i, maps[kind][i // 2] * 2 + i % 2) for i in range(n)])

    def other_core(v):
        return lax.ppermute(v, "loop", [(i, i ^ 1) for i in range(n)])

    x, early, late, gen = pl.pallas_call(
        code_kernel,
        out_shape=(bf16(rows), bf16(half), bf16(half), jax.ShapeDtypeStruct((1, rows), jnp.int32)),
        in_specs=[hbm] * 3,
        out_specs=(vmem,) * 4,
        scratch_shapes=[pltpu.VMEM((1, rows), jnp.int32), pltpu.SemaphoreType.DMA((3,))],
        compiler_params=pltpu.CompilerParams(vmem_limit_bytes=CODE_LIMIT),
        name="code",
    )(embeddings, eligible.reshape(1, rows), generation.reshape(1, rows))

    steps = n // 4
    parts, paths = [[early, late]], [[]]
    held = [parts[0], parts[0]]
    for step in range(steps):
        sent = [held[1], held[0]] if step else held
        paths += [[(kind + k) % 2 for k in range(step + 1)] for kind in (0, 1)][: 1 if step == steps - 1 else 2]
        held = [[None, None], [None, None]]
        for part in (0, 1):
            for kind in (0, 1) if step < steps - 1 else (part,):
                held[kind][part] = swap(kind, sent[kind][part])
        parts += held if step < steps - 1 else [[held[0][0], held[1][1]]]
    across = []
    for k, chunk in enumerate(parts):
        across.append([])
        for part in (0, 1):
            across[k].append(other_core(chunk[part]))
    bits = []
    for i in range(n):
        word = 0
        for k, path in enumerate(paths):
            chip = i // 2
            for kind in path:
                chip = maps[kind][chip]
            for j, source in ((k, chip * 2 + i % 2), (n // 2 + k, chip * 2 + 1 - i % 2)):
                word |= int(source > i) << j
        bits.append(word)
    bits = tuple(bits)
    keys_of = dict(enumerate(parts + across))

    limit = pltpu.CompilerParams(vmem_limit_bytes=8 << 20)

    def score(ids):
        columns = rows * len(ids)
        return pl.pallas_call(
            functools.partial(score_kernel, mult, bits, ids),
            out_shape=(
                jax.ShapeDtypeStruct((rows, columns), jnp.float32),
                jax.ShapeDtypeStruct((rows, rows), jnp.float32),
            ),
            in_specs=[smem] + [vmem] * (2 + 2 * len(ids)),
            out_specs=(vmem, vmem),
            compiler_params=limit,
            cost_estimate=pl.CostEstimate(flops=2 * rows * columns * width, bytes_accessed=0, transcendentals=0),
        )(me, x, gen, *[v for i in ids for v in keys_of[i]])

    chunks = n // 2
    last = chunks - 1
    early_ids = (0, 1, 2, *range(chunks, chunks + 3))
    late_ids = (last - 2, last - 1)
    middle_ids = tuple(i for i in range(3, last - 2)) + tuple(i for i in range(chunks + 3, chunks + last - 2)) + late_ids
    late_ids = tuple(chunks + i for i in late_ids) + (last,)
    plan = (early_ids, middle_ids, late_ids)
    scored = []
    for ids in plan:
        scored.append(score(ids))
    last_ids = (chunks + last,)
    out, peak = pl.pallas_call(
        functools.partial(finish_kernel, mult, bits, tuple(len(ids) for ids in plan), last_ids),
        out_shape=(bf16(rows), jax.ShapeDtypeStruct((1, rows), jnp.float32)),
        in_specs=[smem] + [vmem] * (8 + 4 * chunks),
        out_specs=(vmem, vmem),
        scratch_shapes=[pltpu.VMEM((rows, rows), jnp.float32)],
        compiler_params=limit,
        name="finish",
    )(me, x, gen, *[s for s, _ in scored], *[t for _, t in scored], *[v for ids in (*plan, last_ids) for i in ids for v in keys_of[i]])
    return out, peak.reshape(rows)


def gathered_body(embeddings, generation, eligible):
    _, width = embeddings.shape
    mult = smoothing_divisor / math.sqrt(width)
    keys = lax.all_gather(embeddings, "loop", axis=0, tiled=True)
    key_gen = lax.all_gather(generation, "loop", axis=0, tiled=True)
    key_flag = lax.all_gather(eligible, "loop", axis=0, tiled=True)
    scores = jnp.dot(embeddings, keys.T, preferred_element_type=jnp.float32) * mult
    valid = (key_gen[None, :] < generation[:, None]) & (key_flag[None, :] == 1)
    masked = jnp.where(valid, scores, -jnp.inf)
    peak = jnp.maximum(jnp.max(masked, axis=1), 0.0)
    expo = jnp.where(valid, jnp.exp(scores - peak[:, None]), jnp.float32(0.0))
    total = jnp.exp(-peak) + jnp.sum(expo, axis=1)
    summed = jnp.dot(expo.astype(jnp.bfloat16), keys, preferred_element_type=jnp.float32)
    return (summed / total[:, None]).astype(jnp.bfloat16), peak


def solution(mesh):
    n = mesh.shape["loop"]
    placed = (P(("groups", "loop"), None), P(("groups", "loop")), P(("groups", "loop")))
    small = n <= 16

    def body(*args):
        return ring_body(n, *args) if small else gathered_body(*args)

    return jax.shard_map(
        body,
        mesh=mesh,
        in_specs=placed,
        out_specs=(P(("groups", "loop"), None), P(("groups", "loop"))),
        check_vma=False,
    )
```

profile of v0, /device:TPU:0, one launch (start us, length us, event | category | flops | bytes accessed | tf_op | source)
XLA Modules:
  0.0 43.1 jit_solution(10908419826124508820)
XLA Ops:
  0.6 0.6 %copy-done.3 = s32[128]{0:T(128)S(1)} copy-done((s32[128]{0:T(128)S(1)}, s32[128]{0:T(128)}, u32[]{:S(2)}) %copy-start.3) | copy-done | bytes 536
  1.3 0.0 copy-done.4
  1.3 0.9 %copy-done.2 = bf16[128,1024]{1,0:T(8,128)(2,1)S(1)} copy-done((bf16[128,1024]{1,0:T(8,128)(2,1)S(1)}, bf16[128,1024]{1,0:T(8,128)(2,1)}, u32[]{:S(2)}) %copy-start.2) | copy-done | bytes 262168
  2.3 0.2 code.1
  2.5 0.6 %collective-permute-start.4 = (bf16[64,1024]{1,0:T(8,128)(2,1)S(1)}, bf16[64,1024]{1,0:T(8,128)(2,1)S(1)}, u32[]{:S(2)}, u32[]{:S(2)}) collective-permute-start(bf16[64,1024]{1,0:T(8,128)(2,1)S(1)} %get-tuple-element.16.refs_0_.refs_6_), channel_id=1, source_target_pairs={{0,1},{1,0},{2,3},{3,2},{4,5},{5,4},{6,7},{7,6},{8,9},{9,8},{10,11... | collective-permute-start | bytes 393224 | tf_op jit(solution)/shard_map/ppermute | solution.py:152
  3.0 2.6 %collective-permute-start.2 = (bf16[64,1024]{1,0:T(8,128)(2,1)S(1)}, bf16[64,1024]{1,0:T(8,128)(2,1)S(1)}, u32[]{:S(2)}, u32[]{:S(2)}) collective-permute-start(bf16[64,1024]{1,0:T(8,128)(2,1)S(1)} %get-tuple-element.16.refs_0_.refs_6_), channel_id=1, source_target_pairs={{0,4},{1,5},{2,6},{3,7},{4,0},{5,1},{6,2},{7,3},{8,12},{9,13},{10,... | collective-permute-start | bytes 393224 | tf_op jit(solution)/shard_map/ppermute | solution.py:149
  5.6 1.5 %collective-permute-start = (bf16[64,1024]{1,0:T(8,128)(2,1)S(1)}, bf16[64,1024]{1,0:T(8,128)(2,1)S(1)}, u32[]{:S(2)}, u32[]{:S(2)}) collective-permute-start(bf16[64,1024]{1,0:T(8,128)(2,1)S(1)} %get-tuple-element.16.refs_0_.refs_6_), channel_id=1, source_target_pairs={{0,2},{1,3},{2,0},{3,1},{4,8},{5,9},{6,10},{7,11},{8,4},{9,5},{10,... | collective-permute-start | bytes 393224 | tf_op jit(solution)/shard_map/ppermute | solution.py:149
  7.2 1.6 %collective-permute-start.3 = (bf16[64,1024]{1,0:T(8,128)(2,1)S(1)}, bf16[64,1024]{1,0:T(8,128)(2,1)S(1)}, u32[]{:S(2)}, u32[]{:S(2)}) collective-permute-start(bf16[64,1024]{1,0:T(8,128)(2,1)S(1)} %get-tuple-element.17.refs_1_.refs_7_), channel_id=1, source_target_pairs={{0,4},{1,5},{2,6},{3,7},{4,0},{5,1},{6,2},{7,3},{8,12},{9,13},{10,... | collective-permute-start | bytes 393224 | tf_op jit(solution)/shard_map/ppermute | solution.py:149
  8.8 0.0 collective-permute-done.4.refs_6_.refs_12_
  8.8 1.5 %collective-permute-start.1 = (bf16[64,1024]{1,0:T(8,128)(2,1)S(1)}, bf16[64,1024]{1,0:T(8,128)(2,1)S(1)}, u32[]{:S(2)}, u32[]{:S(2)}) collective-permute-start(bf16[64,1024]{1,0:T(8,128)(2,1)S(1)} %get-tuple-element.17.refs_1_.refs_7_), channel_id=1, source_target_pairs={{0,2},{1,3},{2,0},{3,1},{4,8},{5,9},{6,10},{7,11},{8,4},{9,5},{10,... | collective-permute-start | bytes 393224 | tf_op jit(solution)/shard_map/ppermute | solution.py:149
  10.3 0.0 collective-permute-done.2.refs_4_.refs_10_
  10.3 1.1 %collective-permute-start.10 = (bf16[64,1024]{1,0:T(8,128)(2,1)S(1)}, bf16[64,1024]{1,0:T(8,128)(2,1)S(1)}, u32[]{:S(2)}, u32[]{:S(2)}) collective-permute-start(bf16[64,1024]{1,0:T(8,128)(2,1)S(1)} %collective-permute-done.2.refs_4_.refs_10_), channel_id=1, source_target_pairs={{0,2},{1,3},{2,0},{3,1},{4,8},{5,9},{6,10},{7,11},{8,4},{9,5},{10,... | collective-permute-start | bytes 393224 | tf_op jit(solution)/shard_map/ppermute | solution.py:149
  11.4 0.0 collective-permute-done.refs_2_.refs_8_
  11.4 0.0 collective-permute-start.8
  11.4 0.0 collective-permute-done.5.refs_7_.refs_13_
  11.4 2.2 %collective-permute-start.12 = (bf16[64,1024]{1,0:T(8,128)(2,1)S(1)}, bf16[64,1024]{1,0:T(8,128)(2,1)S(1)}, u32[]{:S(2)}, u32[]{:S(2)}) collective-permute-start(bf16[64,1024]{1,0:T(8,128)(2,1)S(1)} %collective-permute-done.refs_2_.refs_8_), channel_id=1, source_target_pairs={{0,4},{1,5},{2,6},{3,7},{4,0},{5,1},{6,2},{7,3},{8,12},{9,13},{10,... | collective-permute-start | bytes 393224 | tf_op jit(solution)/shard_map/ppermute | solution.py:149
  13.7 0.2 collective-permute-start.6
  13.8 1.3 %collective-permute-done.1.refs_3_.refs_9_ = bf16[64,1024]{1,0:T(8,128)(2,1)S(1)} collective-permute-done((bf16[64,1024]{1,0:T(8,128)(2,1)S(1)}, bf16[64,1024]{1,0:T(8,128)(2,1)S(1)}, u32[]{:S(2)}, u32[]{:S(2)}) %collective-permute-start.1) | collective-permute-done | bytes 131104 | tf_op jit(solution)/shard_map/ppermute | solution.py:149
  15.2 1.5 %collective-permute-start.11 = (bf16[64,1024]{1,0:T(8,128)(2,1)S(1)}, bf16[64,1024]{1,0:T(8,128)(2,1)S(1)}, u32[]{:S(2)}, u32[]{:S(2)}) collective-permute-start(bf16[64,1024]{1,0:T(8,128)(2,1)S(1)} %collective-permute-done.3.refs_5_.refs_11_), channel_id=1, source_target_pairs={{0,2},{1,3},{2,0},{3,1},{4,8},{5,9},{6,10},{7,11},{8,4},{9,5},{10,... | collective-permute-start | bytes 393224 | tf_op jit(solution)/shard_map/ppermute | solution.py:149
  16.7 1.0 %collective-permute-done.10.refs_0_.refs_18_ = bf16[64,1024]{1,0:T(8,128)(2,1)S(1)} collective-permute-done((bf16[64,1024]{1,0:T(8,128)(2,1)S(1)}, bf16[64,1024]{1,0:T(8,128)(2,1)S(1)}, u32[]{:S(2)}, u32[]{:S(2)}) %collective-permute-start.10) | collective-permute-done | bytes 131104 | tf_op jit(solution)/shard_map/ppermute | solution.py:149
  17.7 0.0 collective-permute-start.9
  17.7 0.0 collective-permute-done.8.refs_10_.refs_16_
  17.7 0.6 %collective-permute-start.13 = (bf16[64,1024]{1,0:T(8,128)(2,1)S(1)}, bf16[64,1024]{1,0:T(8,128)(2,1)S(1)}, u32[]{:S(2)}, u32[]{:S(2)}) collective-permute-start(bf16[64,1024]{1,0:T(8,128)(2,1)S(1)} %collective-permute-done.1.refs_3_.refs_9_), channel_id=1, source_target_pairs={{0,4},{1,5},{2,6},{3,7},{4,0},{5,1},{6,2},{7,3},{8,12},{9,13},{10,... | collective-permute-start | bytes 393224 | tf_op jit(solution)/shard_map/ppermute | solution.py:149
  18.3 0.2 collective-permute-start.7
  18.6 0.0 collective-permute-done.6.refs_8_.refs_14_
  18.6 1.4 %collective-permute-start.20 = (bf16[64,1024]{1,0:T(8,128)(2,1)S(1)}, bf16[64,1024]{1,0:T(8,128)(2,1)S(1)}, u32[]{:S(2)}, u32[]{:S(2)}) collective-permute-start(bf16[64,1024]{1,0:T(8,128)(2,1)S(1)} %collective-permute-done.10.refs_0_.refs_18_), channel_id=1, source_target_pairs={{0,4},{1,5},{2,6},{3,7},{4,0},{5,1},{6,2},{7,3},{8,12},{9,13},{10,... | collective-permute-start | bytes 393224 | tf_op jit(solution)/shard_map/ppermute | solution.py:149
  20.0 0.2 collective-permute-done.11.refs_1_.refs_19_
  20.2 1.5 %collective-permute-start.18 = (bf16[64,1024]{1,0:T(8,128)(2,1)S(1)}, bf16[64,1024]{1,0:T(8,128)(2,1)S(1)}, u32[]{:S(2)}, u32[]{:S(2)}) collective-permute-start(bf16[64,1024]{1,0:T(8,128)(2,1)S(1)} %collective-permute-done.12.refs_2_.refs_20_), channel_id=1, source_target_pairs={{0,2},{1,3},{2,0},{3,1},{4,8},{5,9},{6,10},{7,11},{8,4},{9,5},{10,... | collective-permute-start | bytes 393224 | tf_op jit(solution)/shard_map/ppermute | solution.py:149
  21.7 2.4 %collective-permute-done.13.refs_3_.refs_21_ = bf16[64,1024]{1,0:T(8,128)(2,1)S(1)} collective-permute-done((bf16[64,1024]{1,0:T(8,128)(2,1)S(1)}, bf16[64,1024]{1,0:T(8,128)(2,1)S(1)}, u32[]{:S(2)}, u32[]{:S(2)}) %collective-permute-start.13) | collective-permute-done | bytes 131104 | tf_op jit(solution)/shard_map/ppermute | solution.py:149
  24.1 0.6 %collective-permute-start.21 = (bf16[64,1024]{1,0:T(8,128)(2,1)S(1)}, bf16[64,1024]{1,0:T(8,128)(2,1)S(1)}, u32[]{:S(2)}, u32[]{:S(2)}) collective-permute-start(bf16[64,1024]{1,0:T(8,128)(2,1)S(1)} %collective-permute-done.11.refs_1_.refs_19_), channel_id=1, source_target_pairs={{0,4},{1,5},{2,6},{3,7},{4,0},{5,1},{6,2},{7,3},{8,12},{9,13},{10,... | collective-permute-start | bytes 393224 | tf_op jit(solution)/shard_map/ppermute | solution.py:149
  24.7 1.7 %collective-permute-done.20.refs_10_.refs_28_ = bf16[64,1024]{1,0:T(8,128)(2,1)S(1)} collective-permute-done((bf16[64,1024]{1,0:T(8,128)(2,1)S(1)}, bf16[64,1024]{1,0:T(8,128)(2,1)S(1)}, u32[]{:S(2)}, u32[]{:S(2)}) %collective-permute-start.20) | collective-permute-done | bytes 131104 | tf_op jit(solution)/shard_map/ppermute | solution.py:149
  26.4 1.5 %collective-permute-start.19 = (bf16[64,1024]{1,0:T(8,128)(2,1)S(1)}, bf16[64,1024]{1,0:T(8,128)(2,1)S(1)}, u32[]{:S(2)}, u32[]{:S(2)}) collective-permute-start(bf16[64,1024]{1,0:T(8,128)(2,1)S(1)} %collective-permute-done.13.refs_3_.refs_21_), channel_id=1, source_target_pairs={{0,2},{1,3},{2,0},{3,1},{4,8},{5,9},{6,10},{7,11},{8,4},{9,5},{10,... | collective-permute-start | bytes 393224 | tf_op jit(solution)/shard_map/ppermute | solution.py:149
  28.0 0.5 %collective-permute-start.17 = (bf16[64,1024]{1,0:T(8,128)(2,1)S(1)}, bf16[64,1024]{1,0:T(8,128)(2,1)S(1)}, u32[]{:S(2)}, u32[]{:S(2)}) collective-permute-start(bf16[64,1024]{1,0:T(8,128)(2,1)S(1)} %collective-permute-done.13.refs_3_.refs_21_), channel_id=1, source_target_pairs={{0,1},{1,0},{2,3},{3,2},{4,5},{5,4},{6,7},{7,6},{8,9},{9,8},{10,11... | collective-permute-start | bytes 393224 | tf_op jit(solution)/shard_map/ppermute | solution.py:152
  28.5 0.5 %collective-permute-start.26 = (bf16[64,1024]{1,0:T(8,128)(2,1)S(1)}, bf16[64,1024]{1,0:T(8,128)(2,1)S(1)}, u32[]{:S(2)}, u32[]{:S(2)}) collective-permute-start(bf16[64,1024]{1,0:T(8,128)(2,1)S(1)} %collective-permute-done.20.refs_10_.refs_28_), channel_id=1, source_target_pairs={{0,2},{1,3},{2,0},{3,1},{4,8},{5,9},{6,10},{7,11},{8,4},{9,5},{10,... | collective-permute-start | bytes 393224 | tf_op jit(solution)/shard_map/ppermute | solution.py:149
  29.0 1.0 %collective-permute-done.21.refs_11_.refs_29_ = bf16[64,1024]{1,0:T(8,128)(2,1)S(1)} collective-permute-done((bf16[64,1024]{1,0:T(8,128)(2,1)S(1)}, bf16[64,1024]{1,0:T(8,128)(2,1)S(1)}, u32[]{:S(2)}, u32[]{:S(2)}) %collective-permute-start.21) | collective-permute-done | bytes 131104 | tf_op jit(solution)/shard_map/ppermute | solution.py:149
  30.0 1.8 %collective-permute-done.19.refs_9_.refs_27_ = bf16[64,1024]{1,0:T(8,128)(2,1)S(1)} collective-permute-done((bf16[64,1024]{1,0:T(8,128)(2,1)S(1)}, bf16[64,1024]{1,0:T(8,128)(2,1)S(1)}, u32[]{:S(2)}, u32[]{:S(2)}) %collective-permute-start.19) | collective-permute-done | bytes 131104 | tf_op jit(solution)/shard_map/ppermute | solution.py:149
  31.8 0.8 %collective-permute-start.27 = (bf16[64,1024]{1,0:T(8,128)(2,1)S(1)}, bf16[64,1024]{1,0:T(8,128)(2,1)}, u32[]{:S(2)}, u32[]{:S(2)}) collective-permute-start(bf16[64,1024]{1,0:T(8,128)(2,1)S(1)} %collective-permute-done.19.refs_9_.refs_27_), channel_id=1, source_target_pairs={{0,4},{1,5},{2,6},{3,7},{4,0},{5,1},{6,2},{7,3},{8,12},{9,13},{10,... | collective-permute-start | bytes 393224 | tf_op jit(solution)/shard_map/ppermute | solution.py:149
  32.7 0.5 %collective-permute-start.25 = (bf16[64,1024]{1,0:T(8,128)(2,1)S(1)}, bf16[64,1024]{1,0:T(8,128)(2,1)}, u32[]{:S(2)}, u32[]{:S(2)}) collective-permute-start(bf16[64,1024]{1,0:T(8,128)(2,1)S(1)} %collective-permute-done.21.refs_11_.refs_29_), channel_id=1, source_target_pairs={{0,1},{1,0},{2,3},{3,2},{4,5},{5,4},{6,7},{7,6},{8,9},{9,8},{10,11... | collective-permute-start | bytes 393224 | tf_op jit(solution)/shard_map/ppermute | solution.py:152
  33.2 1.1 %collective-permute-done.26.refs_4_.refs_34_ = bf16[64,1024]{1,0:T(8,128)(2,1)S(1)} collective-permute-done((bf16[64,1024]{1,0:T(8,128)(2,1)S(1)}, bf16[64,1024]{1,0:T(8,128)(2,1)S(1)}, u32[]{:S(2)}, u32[]{:S(2)}) %collective-permute-start.26) | collective-permute-done | bytes 131104 | tf_op jit(solution)/shard_map/ppermute | solution.py:149
  34.3 0.7 %copy-done = bf16[64,1024]{1,0:T(8,128)(2,1)} copy-done((bf16[64,1024]{1,0:T(8,128)(2,1)}, bf16[64,1024]{1,0:T(8,128)(2,1)S(1)}, u32[]{:S(2)}) %copy-start) | copy-done | bytes 131096
  35.0 0.5 %collective-permute-start.28 = (bf16[64,1024]{1,0:T(8,128)(2,1)S(1)}, bf16[64,1024]{1,0:T(8,128)(2,1)}, u32[]{:S(2)}, u32[]{:S(2)}) collective-permute-start(bf16[64,1024]{1,0:T(8,128)(2,1)S(1)} %collective-permute-done.26.refs_4_.refs_34_), channel_id=1, source_target_pairs={{0,1},{1,0},{2,3},{3,2},{4,5},{5,4},{6,7},{7,6},{8,9},{9,8},{10,11... | collective-permute-start | bytes 393224 | tf_op jit(solution)/shard_map/ppermute | solution.py:152
  35.5 1.4 %collective-permute-done.27.refs_5_.refs_35_ = bf16[64,1024]{1,0:T(8,128)(2,1)} collective-permute-done((bf16[64,1024]{1,0:T(8,128)(2,1)S(1)}, bf16[64,1024]{1,0:T(8,128)(2,1)}, u32[]{:S(2)}, u32[]{:S(2)}) %collective-permute-start.27) | collective-permute-done | bytes 131104 | tf_op jit(solution)/shard_map/ppermute | solution.py:149
  36.9 0.7 %shard_map.50 = (f32[128,768]{1,0:T(8,128)S(1)}, f32[128,128]{1,0:T(8,128)S(1)}) custom-call(s32[1]{0:T(128)} %bitcast.me_ref, bf16[128,1024]{1,0:T(8,128)(2,1)S(1)} %get-tuple-element.14.x_ref, s32[1,128]{1,0:T(1,128)S(1)} %get-tuple-element.15.gen_ref, bf16[64,1024]{1,0:T(8,128)(2,1)S(1)} %get-tuple-element.16.refs_0_.refs_6_, ...), custom_call_target="tpu_custom_call" | custom-call | flops 201326592 | tf_op jit(solution)/shard_map/pallas_call | solution.py:197
  37.6 0.0 copy-start.1
  37.6 0.7 %shard_map.51 = (f32[128,768]{1,0:T(8,128)S(1)}, f32[128,128]{1,0:T(8,128)S(1)}) custom-call(s32[1]{0:T(128)} %bitcast.me_ref, bf16[128,1024]{1,0:T(8,128)(2,1)S(1)} %get-tuple-element.14.x_ref, s32[1,128]{1,0:T(1,128)S(1)} %get-tuple-element.15.gen_ref, bf16[64,1024]{1,0:T(8,128)(2,1)S(1)} %collective-permute-done.10.refs_0_.refs_18_, ...), custom_call_target="tpu_custom_call" | custom-call | flops 201326592 | tf_op jit(solution)/shard_map/pallas_call | solution.py:197
  38.3 0.2 copy-done.1
  38.5 1.5 %shard_map.52 = (f32[128,384]{1,0:T(8,128)S(1)}, f32[128,128]{1,0:T(8,128)S(1)}) custom-call(s32[1]{0:T(128)} %bitcast.me_ref, bf16[128,1024]{1,0:T(8,128)(2,1)S(1)} %get-tuple-element.14.x_ref, s32[1,128]{1,0:T(1,128)S(1)} %get-tuple-element.15.gen_ref, bf16[64,1024]{1,0:T(8,128)(2,1)} %collective-permute-done.22.refs_0_.refs_30_, ...), custom_call_target="tpu_custom_call" | custom-call | flops 100663296 | tf_op jit(solution)/shard_map/pallas_call | solution.py:197
  40.0 3.1 %finish.1 = (bf16[128,1024]{1,0:T(8,128)(2,1)}, f32[1,128]{1,0:T(1,128)}) custom-call(s32[1]{0:T(128)} %bitcast.me_ref, bf16[128,1024]{1,0:T(8,128)(2,1)S(1)} %get-tuple-element.14.x_ref, s32[1,128]{1,0:T(1,128)S(1)} %get-tuple-element.15.gen_ref, f32[128,768]{1,0:T(8,128)S(1)} %get-tuple-element.18.refs_0_, f32[128,768]{1,0:T(8,128)S(1)} %get-tuple-element.19.refs_1_, ...), custom_call_target="tpu_custom_call" | custom-call | tf_op jit(solution)/shard_map/finish/pallas_call | solution.py:220
  (27 shorter events, 0.1 us)
Async XLA Ops:
  0.6 0.7 %copy-start.3 = (s32[128]{0:T(128)S(1)}, s32[128]{0:T(128)}, u32[]{:S(2)}) copy-start(s32[128]{0:T(128)} %param.5) | copy-start | bytes 1540
  0.6 0.7 %copy-start.4 = (s32[128]{0:T(128)S(1)}, s32[128]{0:T(128)}, u32[]{:S(2)}) copy-start(s32[128]{0:T(128)} %param.4) | copy-start | bytes 1540
  1.3 0.9 %copy-start.2 = (bf16[128,1024]{1,0:T(8,128)(2,1)S(1)}, bf16[128,1024]{1,0:T(8,128)(2,1)}, u32[]{:S(2)}) copy-start(bf16[128,1024]{1,0:T(8,128)(2,1)} %x_hbm.1) | copy-start | bytes 786436
  2.5 6.4 %collective-permute-start.4 = (bf16[64,1024]{1,0:T(8,128)(2,1)S(1)}, bf16[64,1024]{1,0:T(8,128)(2,1)S(1)}, u32[]{:S(2)}, u32[]{:S(2)}) collective-permute-start(bf16[64,1024]{1,0:T(8,128)(2,1)S(1)} %get-tuple-element.16.refs_0_.refs_6_), channel_id=1, source_target_pairs={{0,1},{1,0},{2,3},{3,2},{4,5},{5,4},{6,7},{7,6},{8,9},{9,8},{10,11... | collective-permute-start | bytes 393224 | tf_op jit(solution)/shard_map/ppermute | solution.py:152
  3.0 7.3 %collective-permute-start.2 = (bf16[64,1024]{1,0:T(8,128)(2,1)S(1)}, bf16[64,1024]{1,0:T(8,128)(2,1)S(1)}, u32[]{:S(2)}, u32[]{:S(2)}) collective-permute-start(bf16[64,1024]{1,0:T(8,128)(2,1)S(1)} %get-tuple-element.16.refs_0_.refs_6_), channel_id=1, source_target_pairs={{0,4},{1,5},{2,6},{3,7},{4,0},{5,1},{6,2},{7,3},{8,12},{9,13},{10,... | collective-permute-start | bytes 393224 | tf_op jit(solution)/shard_map/ppermute | solution.py:149
  5.6 5.8 %collective-permute-start = (bf16[64,1024]{1,0:T(8,128)(2,1)S(1)}, bf16[64,1024]{1,0:T(8,128)(2,1)S(1)}, u32[]{:S(2)}, u32[]{:S(2)}) collective-permute-start(bf16[64,1024]{1,0:T(8,128)(2,1)S(1)} %get-tuple-element.16.refs_0_.refs_6_), channel_id=1, source_target_pairs={{0,2},{1,3},{2,0},{3,1},{4,8},{5,9},{6,10},{7,11},{8,4},{9,5},{10,... | collective-permute-start | bytes 393224 | tf_op jit(solution)/shard_map/ppermute | solution.py:149
  7.2 4.3 %collective-permute-start.5 = (bf16[64,1024]{1,0:T(8,128)(2,1)S(1)}, bf16[64,1024]{1,0:T(8,128)(2,1)S(1)}, u32[]{:S(2)}, u32[]{:S(2)}) collective-permute-start(bf16[64,1024]{1,0:T(8,128)(2,1)S(1)} %get-tuple-element.17.refs_1_.refs_7_), channel_id=1, source_target_pairs={{0,1},{1,0},{2,3},{3,2},{4,5},{5,4},{6,7},{7,6},{8,9},{9,8},{10,11... | collective-permute-start | bytes 393224 | tf_op jit(solution)/shard_map/ppermute | solution.py:152
  7.2 6.5 %collective-permute-start.3 = (bf16[64,1024]{1,0:T(8,128)(2,1)S(1)}, bf16[64,1024]{1,0:T(8,128)(2,1)S(1)}, u32[]{:S(2)}, u32[]{:S(2)}) collective-permute-start(bf16[64,1024]{1,0:T(8,128)(2,1)S(1)} %get-tuple-element.17.refs_1_.refs_7_), channel_id=1, source_target_pairs={{0,4},{1,5},{2,6},{3,7},{4,0},{5,1},{6,2},{7,3},{8,12},{9,13},{10,... | collective-permute-start | bytes 393224 | tf_op jit(solution)/shard_map/ppermute | solution.py:149
  8.8 6.4 %collective-permute-start.1 = (bf16[64,1024]{1,0:T(8,128)(2,1)S(1)}, bf16[64,1024]{1,0:T(8,128)(2,1)S(1)}, u32[]{:S(2)}, u32[]{:S(2)}) collective-permute-start(bf16[64,1024]{1,0:T(8,128)(2,1)S(1)} %get-tuple-element.17.refs_1_.refs_7_), channel_id=1, source_target_pairs={{0,2},{1,3},{2,0},{3,1},{4,8},{5,9},{6,10},{7,11},{8,4},{9,5},{10,... | collective-permute-start | bytes 393224 | tf_op jit(solution)/shard_map/ppermute | solution.py:149
  10.3 7.4 %collective-permute-start.10 = (bf16[64,1024]{1,0:T(8,128)(2,1)S(1)}, bf16[64,1024]{1,0:T(8,128)(2,1)S(1)}, u32[]{:S(2)}, u32[]{:S(2)}) collective-permute-start(bf16[64,1024]{1,0:T(8,128)(2,1)S(1)} %collective-permute-done.2.refs_4_.refs_10_), channel_id=1, source_target_pairs={{0,2},{1,3},{2,0},{3,1},{4,8},{5,9},{6,10},{7,11},{8,4},{9,5},{10,... | collective-permute-start | bytes 393224 | tf_op jit(solution)/shard_map/ppermute | solution.py:149
  11.4 6.3 %collective-permute-start.8 = (bf16[64,1024]{1,0:T(8,128)(2,1)S(1)}, bf16[64,1024]{1,0:T(8,128)(2,1)S(1)}, u32[]{:S(2)}, u32[]{:S(2)}) collective-permute-start(bf16[64,1024]{1,0:T(8,128)(2,1)S(1)} %collective-permute-done.2.refs_4_.refs_10_), channel_id=1, source_target_pairs={{0,1},{1,0},{2,3},{3,2},{4,5},{5,4},{6,7},{7,6},{8,9},{9,8},{10,11... | collective-permute-start | bytes 393224 | tf_op jit(solution)/shard_map/ppermute | solution.py:152
  11.4 6.9 %collective-permute-start.12 = (bf16[64,1024]{1,0:T(8,128)(2,1)S(1)}, bf16[64,1024]{1,0:T(8,128)(2,1)S(1)}, u32[]{:S(2)}, u32[]{:S(2)}) collective-permute-start(bf16[64,1024]{1,0:T(8,128)(2,1)S(1)} %collective-permute-done.refs_2_.refs_8_), channel_id=1, source_target_pairs={{0,4},{1,5},{2,6},{3,7},{4,0},{5,1},{6,2},{7,3},{8,12},{9,13},{10,... | collective-permute-start | bytes 393224 | tf_op jit(solution)/shard_map/ppermute | solution.py:149
  13.7 4.9 %collective-permute-start.6 = (bf16[64,1024]{1,0:T(8,128)(2,1)S(1)}, bf16[64,1024]{1,0:T(8,128)(2,1)S(1)}, u32[]{:S(2)}, u32[]{:S(2)}) collective-permute-start(bf16[64,1024]{1,0:T(8,128)(2,1)S(1)} %collective-permute-done.refs_2_.refs_8_), channel_id=1, source_target_pairs={{0,1},{1,0},{2,3},{3,2},{4,5},{5,4},{6,7},{7,6},{8,9},{9,8},{10,11... | collective-permute-start | bytes 393224 | tf_op jit(solution)/shard_map/ppermute | solution.py:152
  15.2 5.0 %collective-permute-start.11 = (bf16[64,1024]{1,0:T(8,128)(2,1)S(1)}, bf16[64,1024]{1,0:T(8,128)(2,1)S(1)}, u32[]{:S(2)}, u32[]{:S(2)}) collective-permute-start(bf16[64,1024]{1,0:T(8,128)(2,1)S(1)} %collective-permute-done.3.refs_5_.refs_11_), channel_id=1, source_target_pairs={{0,2},{1,3},{2,0},{3,1},{4,8},{5,9},{6,10},{7,11},{8,4},{9,5},{10,... | collective-permute-start | bytes 393224 | tf_op jit(solution)/shard_map/ppermute | solution.py:149
  17.7 2.4 %collective-permute-start.9 = (bf16[64,1024]{1,0:T(8,128)(2,1)S(1)}, bf16[64,1024]{1,0:T(8,128)(2,1)S(1)}, u32[]{:S(2)}, u32[]{:S(2)}) collective-permute-start(bf16[64,1024]{1,0:T(8,128)(2,1)S(1)} %collective-permute-done.3.refs_5_.refs_11_), channel_id=1, source_target_pairs={{0,1},{1,0},{2,3},{3,2},{4,5},{5,4},{6,7},{7,6},{8,9},{9,8},{10,11... | collective-permute-start | bytes 393224 | tf_op jit(solution)/shard_map/ppermute | solution.py:152
  17.7 6.4 %collective-permute-start.13 = (bf16[64,1024]{1,0:T(8,128)(2,1)S(1)}, bf16[64,1024]{1,0:T(8,128)(2,1)S(1)}, u32[]{:S(2)}, u32[]{:S(2)}) collective-permute-start(bf16[64,1024]{1,0:T(8,128)(2,1)S(1)} %collective-permute-done.1.refs_3_.refs_9_), channel_id=1, source_target_pairs={{0,4},{1,5},{2,6},{3,7},{4,0},{5,1},{6,2},{7,3},{8,12},{9,13},{10,... | collective-permute-start | bytes 393224 | tf_op jit(solution)/shard_map/ppermute | solution.py:149
  18.3 5.8 %collective-permute-start.7 = (bf16[64,1024]{1,0:T(8,128)(2,1)S(1)}, bf16[64,1024]{1,0:T(8,128)(2,1)S(1)}, u32[]{:S(2)}, u32[]{:S(2)}) collective-permute-start(bf16[64,1024]{1,0:T(8,128)(2,1)S(1)} %collective-permute-done.1.refs_3_.refs_9_), channel_id=1, source_target_pairs={{0,1},{1,0},{2,3},{3,2},{4,5},{5,4},{6,7},{7,6},{8,9},{9,8},{10,11... | collective-permute-start | bytes 393224 | tf_op jit(solution)/shard_map/ppermute | solution.py:152
  18.6 7.9 %collective-permute-start.20 = (bf16[64,1024]{1,0:T(8,128)(2,1)S(1)}, bf16[64,1024]{1,0:T(8,128)(2,1)S(1)}, u32[]{:S(2)}, u32[]{:S(2)}) collective-permute-start(bf16[64,1024]{1,0:T(8,128)(2,1)S(1)} %collective-permute-done.10.refs_0_.refs_18_), channel_id=1, source_target_pairs={{0,4},{1,5},{2,6},{3,7},{4,0},{5,1},{6,2},{7,3},{8,12},{9,13},{10,... | collective-permute-start | bytes 393224 | tf_op jit(solution)/shard_map/ppermute | solution.py:149
  20.1 7.8 %collective-permute-start.14 = (bf16[64,1024]{1,0:T(8,128)(2,1)S(1)}, bf16[64,1024]{1,0:T(8,128)(2,1)S(1)}, u32[]{:S(2)}, u32[]{:S(2)}) collective-permute-start(bf16[64,1024]{1,0:T(8,128)(2,1)S(1)} %collective-permute-done.10.refs_0_.refs_18_), channel_id=1, source_target_pairs={{0,1},{1,0},{2,3},{3,2},{4,5},{5,4},{6,7},{7,6},{8,9},{9,8},{10,11... | collective-permute-start | bytes 393224 | tf_op jit(solution)/shard_map/ppermute | solution.py:152
  20.2 7.8 %collective-permute-start.18 = (bf16[64,1024]{1,0:T(8,128)(2,1)S(1)}, bf16[64,1024]{1,0:T(8,128)(2,1)S(1)}, u32[]{:S(2)}, u32[]{:S(2)}) collective-permute-start(bf16[64,1024]{1,0:T(8,128)(2,1)S(1)} %collective-permute-done.12.refs_2_.refs_20_), channel_id=1, source_target_pairs={{0,2},{1,3},{2,0},{3,1},{4,8},{5,9},{6,10},{7,11},{8,4},{9,5},{10,... | collective-permute-start | bytes 393224 | tf_op jit(solution)/shard_map/ppermute | solution.py:149
  24.1 4.4 %collective-permute-start.16 = (bf16[64,1024]{1,0:T(8,128)(2,1)S(1)}, bf16[64,1024]{1,0:T(8,128)(2,1)S(1)}, u32[]{:S(2)}, u32[]{:S(2)}) collective-permute-start(bf16[64,1024]{1,0:T(8,128)(2,1)S(1)} %collective-permute-done.12.refs_2_.refs_20_), channel_id=1, source_target_pairs={{0,1},{1,0},{2,3},{3,2},{4,5},{5,4},{6,7},{7,6},{8,9},{9,8},{10,11... | collective-permute-start | bytes 393224 | tf_op jit(solution)/shard_map/ppermute | solution.py:152
  24.1 5.9 %collective-permute-start.21 = (bf16[64,1024]{1,0:T(8,128)(2,1)S(1)}, bf16[64,1024]{1,0:T(8,128)(2,1)S(1)}, u32[]{:S(2)}, u32[]{:S(2)}) collective-permute-start(bf16[64,1024]{1,0:T(8,128)(2,1)S(1)} %collective-permute-done.11.refs_1_.refs_19_), channel_id=1, source_target_pairs={{0,4},{1,5},{2,6},{3,7},{4,0},{5,1},{6,2},{7,3},{8,12},{9,13},{10,... | collective-permute-start | bytes 393224 | tf_op jit(solution)/shard_map/ppermute | solution.py:149
  26.4 5.4 %collective-permute-start.19 = (bf16[64,1024]{1,0:T(8,128)(2,1)S(1)}, bf16[64,1024]{1,0:T(8,128)(2,1)S(1)}, u32[]{:S(2)}, u32[]{:S(2)}) collective-permute-start(bf16[64,1024]{1,0:T(8,128)(2,1)S(1)} %collective-permute-done.13.refs_3_.refs_21_), channel_id=1, source_target_pairs={{0,2},{1,3},{2,0},{3,1},{4,8},{5,9},{6,10},{7,11},{8,4},{9,5},{10,... | collective-permute-start | bytes 393224 | tf_op jit(solution)/shard_map/ppermute | solution.py:149
  28.0 4.7 %collective-permute-start.15 = (bf16[64,1024]{1,0:T(8,128)(2,1)S(1)}, bf16[64,1024]{1,0:T(8,128)(2,1)S(1)}, u32[]{:S(2)}, u32[]{:S(2)}) collective-permute-start(bf16[64,1024]{1,0:T(8,128)(2,1)S(1)} %collective-permute-done.11.refs_1_.refs_19_), channel_id=1, source_target_pairs={{0,1},{1,0},{2,3},{3,2},{4,5},{5,4},{6,7},{7,6},{8,9},{9,8},{10,11... | collective-permute-start | bytes 393224 | tf_op jit(solution)/shard_map/ppermute | solution.py:152
  28.0 4.7 %collective-permute-start.17 = (bf16[64,1024]{1,0:T(8,128)(2,1)S(1)}, bf16[64,1024]{1,0:T(8,128)(2,1)S(1)}, u32[]{:S(2)}, u32[]{:S(2)}) collective-permute-start(bf16[64,1024]{1,0:T(8,128)(2,1)S(1)} %collective-permute-done.13.refs_3_.refs_21_), channel_id=1, source_target_pairs={{0,1},{1,0},{2,3},{3,2},{4,5},{5,4},{6,7},{7,6},{8,9},{9,8},{10,11... | collective-permute-start | bytes 393224 | tf_op jit(solution)/shard_map/ppermute | solution.py:152
  28.5 5.8 %collective-permute-start.26 = (bf16[64,1024]{1,0:T(8,128)(2,1)S(1)}, bf16[64,1024]{1,0:T(8,128)(2,1)S(1)}, u32[]{:S(2)}, u32[]{:S(2)}) collective-permute-start(bf16[64,1024]{1,0:T(8,128)(2,1)S(1)} %collective-permute-done.20.refs_10_.refs_28_), channel_id=1, source_target_pairs={{0,2},{1,3},{2,0},{3,1},{4,8},{5,9},{6,10},{7,11},{8,4},{9,5},{10,... | collective-permute-start | bytes 393224 | tf_op jit(solution)/shard_map/ppermute | solution.py:149
  30.0 4.3 %collective-permute-start.24 = (bf16[64,1024]{1,0:T(8,128)(2,1)S(1)}, bf16[64,1024]{1,0:T(8,128)(2,1)S(1)}, u32[]{:S(2)}, u32[]{:S(2)}) collective-permute-start(bf16[64,1024]{1,0:T(8,128)(2,1)S(1)} %collective-permute-done.20.refs_10_.refs_28_), channel_id=1, source_target_pairs={{0,1},{1,0},{2,3},{3,2},{4,5},{5,4},{6,7},{7,6},{8,9},{9,8},{10,11... | collective-permute-start | bytes 393224 | tf_op jit(solution)/shard_map/ppermute | solution.py:152
  31.8 5.1 %collective-permute-start.27 = (bf16[64,1024]{1,0:T(8,128)(2,1)S(1)}, bf16[64,1024]{1,0:T(8,128)(2,1)}, u32[]{:S(2)}, u32[]{:S(2)}) collective-permute-start(bf16[64,1024]{1,0:T(8,128)(2,1)S(1)} %collective-permute-done.19.refs_9_.refs_27_), channel_id=1, source_target_pairs={{0,4},{1,5},{2,6},{3,7},{4,0},{5,1},{6,2},{7,3},{8,12},{9,13},{10,... | collective-permute-start | bytes 393224 | tf_op jit(solution)/shard_map/ppermute | solution.py:149
  32.7 5.6 %collective-permute-start.22 = (bf16[64,1024]{1,0:T(8,128)(2,1)S(1)}, bf16[64,1024]{1,0:T(8,128)(2,1)}, u32[]{:S(2)}, u32[]{:S(2)}) collective-permute-start(bf16[64,1024]{1,0:T(8,128)(2,1)S(1)} %collective-permute-done.18.refs_8_.refs_26_), channel_id=1, source_target_pairs={{0,1},{1,0},{2,3},{3,2},{4,5},{5,4},{6,7},{7,6},{8,9},{9,8},{10,11... | collective-permute-start | bytes 393224 | tf_op jit(solution)/shard_map/ppermute | solution.py:152
  32.7 5.6 %collective-permute-start.25 = (bf16[64,1024]{1,0:T(8,128)(2,1)S(1)}, bf16[64,1024]{1,0:T(8,128)(2,1)}, u32[]{:S(2)}, u32[]{:S(2)}) collective-permute-start(bf16[64,1024]{1,0:T(8,128)(2,1)S(1)} %collective-permute-done.21.refs_11_.refs_29_), channel_id=1, source_target_pairs={{0,1},{1,0},{2,3},{3,2},{4,5},{5,4},{6,7},{7,6},{8,9},{9,8},{10,11... | collective-permute-start | bytes 393224 | tf_op jit(solution)/shard_map/ppermute | solution.py:152
  34.3 4.0 %collective-permute-start.23 = (bf16[64,1024]{1,0:T(8,128)(2,1)S(1)}, bf16[64,1024]{1,0:T(8,128)(2,1)}, u32[]{:S(2)}, u32[]{:S(2)}) collective-permute-start(bf16[64,1024]{1,0:T(8,128)(2,1)S(1)} %collective-permute-done.19.refs_9_.refs_27_), channel_id=1, source_target_pairs={{0,1},{1,0},{2,3},{3,2},{4,5},{5,4},{6,7},{7,6},{8,9},{9,8},{10,11... | collective-permute-start | bytes 393224 | tf_op jit(solution)/shard_map/ppermute | solution.py:152
  34.3 0.7 %copy-start = (bf16[64,1024]{1,0:T(8,128)(2,1)}, bf16[64,1024]{1,0:T(8,128)(2,1)S(1)}, u32[]{:S(2)}) copy-start(bf16[64,1024]{1,0:T(8,128)(2,1)S(1)} %collective-permute-done.24.refs_2_.refs_32_) | copy-start | bytes 393220
  35.0 5.0 %collective-permute-start.28 = (bf16[64,1024]{1,0:T(8,128)(2,1)S(1)}, bf16[64,1024]{1,0:T(8,128)(2,1)}, u32[]{:S(2)}, u32[]{:S(2)}) collective-permute-start(bf16[64,1024]{1,0:T(8,128)(2,1)S(1)} %collective-permute-done.26.refs_4_.refs_34_), channel_id=1, source_target_pairs={{0,1},{1,0},{2,3},{3,2},{4,5},{5,4},{6,7},{7,6},{8,9},{9,8},{10,11... | collective-permute-start | bytes 393224 | tf_op jit(solution)/shard_map/ppermute | solution.py:152
  36.9 3.1 %collective-permute-start.29 = (bf16[64,1024]{1,0:T(8,128)(2,1)}, bf16[64,1024]{1,0:T(8,128)(2,1)}, u32[]{:S(2)}, u32[]{:S(2)}) collective-permute-start(bf16[64,1024]{1,0:T(8,128)(2,1)} %collective-permute-done.27.refs_5_.refs_35_), channel_id=1, source_target_pairs={{0,1},{1,0},{2,3},{3,2},{4,5},{5,4},{6,7},{7,6},{8,9},{9,8},{10,11... | collective-permute-start | bytes 393224 | tf_op jit(solution)/shard_map/ppermute | solution.py:152
  37.6 0.9 %copy-start.1 = (bf16[64,1024]{1,0:T(8,128)(2,1)S(1)}, bf16[64,1024]{1,0:T(8,128)(2,1)}, u32[]{:S(2)}) copy-start(bf16[64,1024]{1,0:T(8,128)(2,1)} %copy-done) | copy-start | bytes 393220
where the time goes:
time: 43.5 us; the launch traced here: 43.1 us
  starting transfers between devices  21.7 us (50%)
  waiting for transfers between devices  12.1 us (28%)
  Pallas kernels  6.15 us (14%)
  local copies, waits for them, and re-layouts  2.45 us (6%)
  between operations  0.76 us (2%)
    ppermute x14, starting transfers between devices, swap(): lax.ppermute(v, 'loop', [(i, maps[kind][i // 2] * 2 + i % 2) for i in ran...  19.2 us
    ppermute x14, waiting for transfers between devices, swap(): lax.ppermute(v, 'loop', [(i, maps[kind][i // 2] * 2 + i % 2) for i in ran...  12.1 us
    pallas_call x1, Pallas kernels, ring_body(): pl.pallas_call(functools.partial(finish_kernel, mult, bits, tuple((len(id...  3.14 us
    pallas_call x3, Pallas kernels, score(): pl.pallas_call(functools.partial(score_kernel, mult, bits, ids), out_shap...  2.82 us
    ppermute x16, starting transfers between devices, other_core(): return lax.ppermute(v, 'loop', [(i, i ^ 1) for i in range(n)])  2.49 us
    unnamed x10, local copies, waits for them, and re-layouts  2.45 us
  transfers between devices with their start and end apart: 30, of which 9 were waited for; matrix products, arithmetic and copies ran while one was open for 0% of the time, Pallas kernels for 7%

commit v1 on v0

--- a/solution.py
+++ b/solution.py
@@ -115,12 +115,12 @@
     total = jnp.exp(-peak)
     acc = [None, None]
     edge = 2 * rows
-    for k in range(0, len(pieces), 2):
-        s = jnp.concatenate([ref[:, at : at + rows] for ref, at in pieces[k : k + 2]], axis=1)
+    for k in range(0, len(pieces), 16):
+        s = jnp.concatenate([ref[:, at : at + rows] for ref, at in pieces[k : k + 16]], axis=1)
         expo = jnp.exp(s - peak)
         total = total + jnp.sum(expo, axis=1, keepdims=True)
         w = expo.astype(jnp.bfloat16)
-        quad = keys[2 * k : 2 * k + 4]
+        quad = keys[2 * k : 2 * k + 32]
         head = jnp.concatenate([v[:, :edge] for v in quad], axis=0)
         head = jnp.where(head == head, head, jnp.zeros_like(head))
         tail = jnp.concatenate([v[:, edge:] for v in quad], axis=0)

time: 43.5 us -> 43.5 us (level)
  no operation moved by 1% of the time
where the time goes in v1:
time: 43.5 us; the launch traced here: 43.1 us
  starting transfers between devices  21.7 us (50%)
  waiting for transfers between devices  12.1 us (28%)
  Pallas kernels  6.07 us (14%)
  local copies, waits for them, and re-layouts  2.45 us (6%)
  between operations  0.76 us (2%)
    ppermute x14, starting transfers between devices, swap(): lax.ppermute(v, 'loop', [(i, maps[kind][i // 2] * 2 + i % 2) for i in ran...  19.2 us
    ppermute x14, waiting for transfers between devices, swap(): lax.ppermute(v, 'loop', [(i, maps[kind][i // 2] * 2 + i % 2) for i in ran...  12.1 us
    pallas_call x1, Pallas kernels, ring_body(): pl.pallas_call(functools.partial(finish_kernel, mult, bits, tuple((len(id...  3.06 us
    pallas_call x3, Pallas kernels, score(): pl.pallas_call(functools.partial(score_kernel, mult, bits, ids), out_shap...  2.82 us
    ppermute x16, starting transfers between devices, other_core(): return lax.ppermute(v, 'loop', [(i, i ^ 1) for i in range(n)])  2.49 us
    unnamed x10, local copies, waits for them, and re-layouts  2.45 us
  transfers between devices with their start and end apart: 30, of which 9 were waited for; matrix products, arithmetic and copies ran while one was open for 0% of the time, Pallas kernels for 7%

profile of v1, /device:TPU:0, one launch (start us, length us, event | category | flops | bytes accessed | tf_op | source)
XLA Modules:
  0.0 43.1 jit_solution(14119224400100482411)
XLA Ops:
  0.6 0.6 %copy-done.3 = s32[128]{0:T(128)S(1)} copy-done((s32[128]{0:T(128)S(1)}, s32[128]{0:T(128)}, u32[]{:S(2)}) %copy-start.3) | copy-done | bytes 536
  1.3 0.0 copy-done.4
  1.3 0.9 %copy-done.2 = bf16[128,1024]{1,0:T(8,128)(2,1)S(1)} copy-done((bf16[128,1024]{1,0:T(8,128)(2,1)S(1)}, bf16[128,1024]{1,0:T(8,128)(2,1)}, u32[]{:S(2)}) %copy-start.2) | copy-done | bytes 262168
  2.3 0.2 code.1
  2.5 0.6 %collective-permute-start.4 = (bf16[64,1024]{1,0:T(8,128)(2,1)S(1)}, bf16[64,1024]{1,0:T(8,128)(2,1)S(1)}, u32[]{:S(2)}, u32[]{:S(2)}) collective-permute-start(bf16[64,1024]{1,0:T(8,128)(2,1)S(1)} %get-tuple-element.16.refs_0_.refs_6_), channel_id=1, source_target_pairs={{0,1},{1,0},{2,3},{3,2},{4,5},{5,4},{6,7},{7,6},{8,9},{9,8},{10,11... | collective-permute-start | bytes 393224 | tf_op jit(solution)/shard_map/ppermute | solution.py:152
  3.0 2.6 %collective-permute-start.2 = (bf16[64,1024]{1,0:T(8,128)(2,1)S(1)}, bf16[64,1024]{1,0:T(8,128)(2,1)S(1)}, u32[]{:S(2)}, u32[]{:S(2)}) collective-permute-start(bf16[64,1024]{1,0:T(8,128)(2,1)S(1)} %get-tuple-element.16.refs_0_.refs_6_), channel_id=1, source_target_pairs={{0,4},{1,5},{2,6},{3,7},{4,0},{5,1},{6,2},{7,3},{8,12},{9,13},{10,... | collective-permute-start | bytes 393224 | tf_op jit(solution)/shard_map/ppermute | solution.py:149
  5.6 1.5 %collective-permute-start = (bf16[64,1024]{1,0:T(8,128)(2,1)S(1)}, bf16[64,1024]{1,0:T(8,128)(2,1)S(1)}, u32[]{:S(2)}, u32[]{:S(2)}) collective-permute-start(bf16[64,1024]{1,0:T(8,128)(2,1)S(1)} %get-tuple-element.16.refs_0_.refs_6_), channel_id=1, source_target_pairs={{0,2},{1,3},{2,0},{3,1},{4,8},{5,9},{6,10},{7,11},{8,4},{9,5},{10,... | collective-permute-start | bytes 393224 | tf_op jit(solution)/shard_map/ppermute | solution.py:149
  7.2 1.6 %collective-permute-start.3 = (bf16[64,1024]{1,0:T(8,128)(2,1)S(1)}, bf16[64,1024]{1,0:T(8,128)(2,1)S(1)}, u32[]{:S(2)}, u32[]{:S(2)}) collective-permute-start(bf16[64,1024]{1,0:T(8,128)(2,1)S(1)} %get-tuple-element.17.refs_1_.refs_7_), channel_id=1, source_target_pairs={{0,4},{1,5},{2,6},{3,7},{4,0},{5,1},{6,2},{7,3},{8,12},{9,13},{10,... | collective-permute-start | bytes 393224 | tf_op jit(solution)/shard_map/ppermute | solution.py:149
  8.8 0.0 collective-permute-done.4.refs_6_.refs_12_
  8.8 1.5 %collective-permute-start.1 = (bf16[64,1024]{1,0:T(8,128)(2,1)S(1)}, bf16[64,1024]{1,0:T(8,128)(2,1)S(1)}, u32[]{:S(2)}, u32[]{:S(2)}) collective-permute-start(bf16[64,1024]{1,0:T(8,128)(2,1)S(1)} %get-tuple-element.17.refs_1_.refs_7_), channel_id=1, source_target_pairs={{0,2},{1,3},{2,0},{3,1},{4,8},{5,9},{6,10},{7,11},{8,4},{9,5},{10,... | collective-permute-start | bytes 393224 | tf_op jit(solution)/shard_map/ppermute | solution.py:149
  10.3 0.0 collective-permute-done.2.refs_4_.refs_10_
  10.3 1.1 %collective-permute-start.10 = (bf16[64,1024]{1,0:T(8,128)(2,1)S(1)}, bf16[64,1024]{1,0:T(8,128)(2,1)S(1)}, u32[]{:S(2)}, u32[]{:S(2)}) collective-permute-start(bf16[64,1024]{1,0:T(8,128)(2,1)S(1)} %collective-permute-done.2.refs_4_.refs_10_), channel_id=1, source_target_pairs={{0,2},{1,3},{2,0},{3,1},{4,8},{5,9},{6,10},{7,11},{8,4},{9,5},{10,... | collective-permute-start | bytes 393224 | tf_op jit(solution)/shard_map/ppermute | solution.py:149
  11.4 0.0 collective-permute-done.refs_2_.refs_8_
  11.4 0.0 collective-permute-start.8
  11.4 0.0 collective-permute-done.5.refs_7_.refs_13_
  11.4 2.2 %collective-permute-start.12 = (bf16[64,1024]{1,0:T(8,128)(2,1)S(1)}, bf16[64,1024]{1,0:T(8,128)(2,1)S(1)}, u32[]{:S(2)}, u32[]{:S(2)}) collective-permute-start(bf16[64,1024]{1,0:T(8,128)(2,1)S(1)} %collective-permute-done.refs_2_.refs_8_), channel_id=1, source_target_pairs={{0,4},{1,5},{2,6},{3,7},{4,0},{5,1},{6,2},{7,3},{8,12},{9,13},{10,... | collective-permute-start | bytes 393224 | tf_op jit(solution)/shard_map/ppermute | solution.py:149
  13.7 0.2 collective-permute-start.6
  13.8 1.3 %collective-permute-done.1.refs_3_.refs_9_ = bf16[64,1024]{1,0:T(8,128)(2,1)S(1)} collective-permute-done((bf16[64,1024]{1,0:T(8,128)(2,1)S(1)}, bf16[64,1024]{1,0:T(8,128)(2,1)S(1)}, u32[]{:S(2)}, u32[]{:S(2)}) %collective-permute-start.1) | collective-permute-done | bytes 131104 | tf_op jit(solution)/shard_map/ppermute | solution.py:149
  15.2 1.5 %collective-permute-start.11 = (bf16[64,1024]{1,0:T(8,128)(2,1)S(1)}, bf16[64,1024]{1,0:T(8,128)(2,1)S(1)}, u32[]{:S(2)}, u32[]{:S(2)}) collective-permute-start(bf16[64,1024]{1,0:T(8,128)(2,1)S(1)} %collective-permute-done.3.refs_5_.refs_11_), channel_id=1, source_target_pairs={{0,2},{1,3},{2,0},{3,1},{4,8},{5,9},{6,10},{7,11},{8,4},{9,5},{10,... | collective-permute-start | bytes 393224 | tf_op jit(solution)/shard_map/ppermute | solution.py:149
  16.7 1.0 %collective-permute-done.10.refs_0_.refs_18_ = bf16[64,1024]{1,0:T(8,128)(2,1)S(1)} collective-permute-done((bf16[64,1024]{1,0:T(8,128)(2,1)S(1)}, bf16[64,1024]{1,0:T(8,128)(2,1)S(1)}, u32[]{:S(2)}, u32[]{:S(2)}) %collective-permute-start.10) | collective-permute-done | bytes 131104 | tf_op jit(solution)/shard_map/ppermute | solution.py:149
  17.7 0.0 collective-permute-start.9
  17.7 0.0 collective-permute-done.8.refs_10_.refs_16_
  17.7 0.6 %collective-permute-start.13 = (bf16[64,1024]{1,0:T(8,128)(2,1)S(1)}, bf16[64,1024]{1,0:T(8,128)(2,1)S(1)}, u32[]{:S(2)}, u32[]{:S(2)}) collective-permute-start(bf16[64,1024]{1,0:T(8,128)(2,1)S(1)} %collective-permute-done.1.refs_3_.refs_9_), channel_id=1, source_target_pairs={{0,4},{1,5},{2,6},{3,7},{4,0},{5,1},{6,2},{7,3},{8,12},{9,13},{10,... | collective-permute-start | bytes 393224 | tf_op jit(solution)/shard_map/ppermute | solution.py:149
  18.3 0.2 collective-permute-start.7
  18.6 0.0 collective-permute-done.6.refs_8_.refs_14_
  18.6 1.4 %collective-permute-start.20 = (bf16[64,1024]{1,0:T(8,128)(2,1)S(1)}, bf16[64,1024]{1,0:T(8,128)(2,1)S(1)}, u32[]{:S(2)}, u32[]{:S(2)}) collective-permute-start(bf16[64,1024]{1,0:T(8,128)(2,1)S(1)} %collective-permute-done.10.refs_0_.refs_18_), channel_id=1, source_target_pairs={{0,4},{1,5},{2,6},{3,7},{4,0},{5,1},{6,2},{7,3},{8,12},{9,13},{10,... | collective-permute-start | bytes 393224 | tf_op jit(solution)/shard_map/ppermute | solution.py:149
  20.0 0.2 collective-permute-done.11.refs_1_.refs_19_
  20.2 1.5 %collective-permute-start.18 = (bf16[64,1024]{1,0:T(8,128)(2,1)S(1)}, bf16[64,1024]{1,0:T(8,128)(2,1)S(1)}, u32[]{:S(2)}, u32[]{:S(2)}) collective-permute-start(bf16[64,1024]{1,0:T(8,128)(2,1)S(1)} %collective-permute-done.12.refs_2_.refs_20_), channel_id=1, source_target_pairs={{0,2},{1,3},{2,0},{3,1},{4,8},{5,9},{6,10},{7,11},{8,4},{9,5},{10,... | collective-permute-start | bytes 393224 | tf_op jit(solution)/shard_map/ppermute | solution.py:149
  21.7 2.4 %collective-permute-done.13.refs_3_.refs_21_ = bf16[64,1024]{1,0:T(8,128)(2,1)S(1)} collective-permute-done((bf16[64,1024]{1,0:T(8,128)(2,1)S(1)}, bf16[64,1024]{1,0:T(8,128)(2,1)S(1)}, u32[]{:S(2)}, u32[]{:S(2)}) %collective-permute-start.13) | collective-permute-done | bytes 131104 | tf_op jit(solution)/shard_map/ppermute | solution.py:149
  24.1 0.6 %collective-permute-start.21 = (bf16[64,1024]{1,0:T(8,128)(2,1)S(1)}, bf16[64,1024]{1,0:T(8,128)(2,1)S(1)}, u32[]{:S(2)}, u32[]{:S(2)}) collective-permute-start(bf16[64,1024]{1,0:T(8,128)(2,1)S(1)} %collective-permute-done.11.refs_1_.refs_19_), channel_id=1, source_target_pairs={{0,4},{1,5},{2,6},{3,7},{4,0},{5,1},{6,2},{7,3},{8,12},{9,13},{10,... | collective-permute-start | bytes 393224 | tf_op jit(solution)/shard_map/ppermute | solution.py:149
  24.7 1.7 %collective-permute-done.20.refs_10_.refs_28_ = bf16[64,1024]{1,0:T(8,128)(2,1)S(1)} collective-permute-done((bf16[64,1024]{1,0:T(8,128)(2,1)S(1)}, bf16[64,1024]{1,0:T(8,128)(2,1)S(1)}, u32[]{:S(2)}, u32[]{:S(2)}) %collective-permute-start.20) | collective-permute-done | bytes 131104 | tf_op jit(solution)/shard_map/ppermute | solution.py:149
  26.4 1.5 %collective-permute-start.19 = (bf16[64,1024]{1,0:T(8,128)(2,1)S(1)}, bf16[64,1024]{1,0:T(8,128)(2,1)S(1)}, u32[]{:S(2)}, u32[]{:S(2)}) collective-permute-start(bf16[64,1024]{1,0:T(8,128)(2,1)S(1)} %collective-permute-done.13.refs_3_.refs_21_), channel_id=1, source_target_pairs={{0,2},{1,3},{2,0},{3,1},{4,8},{5,9},{6,10},{7,11},{8,4},{9,5},{10,... | collective-permute-start | bytes 393224 | tf_op jit(solution)/shard_map/ppermute | solution.py:149
  28.0 0.5 %collective-permute-start.17 = (bf16[64,1024]{1,0:T(8,128)(2,1)S(1)}, bf16[64,1024]{1,0:T(8,128)(2,1)S(1)}, u32[]{:S(2)}, u32[]{:S(2)}) collective-permute-start(bf16[64,1024]{1,0:T(8,128)(2,1)S(1)} %collective-permute-done.13.refs_3_.refs_21_), channel_id=1, source_target_pairs={{0,1},{1,0},{2,3},{3,2},{4,5},{5,4},{6,7},{7,6},{8,9},{9,8},{10,11... | collective-permute-start | bytes 393224 | tf_op jit(solution)/shard_map/ppermute | solution.py:152
  28.5 0.5 %collective-permute-start.26 = (bf16[64,1024]{1,0:T(8,128)(2,1)S(1)}, bf16[64,1024]{1,0:T(8,128)(2,1)S(1)}, u32[]{:S(2)}, u32[]{:S(2)}) collective-permute-start(bf16[64,1024]{1,0:T(8,128)(2,1)S(1)} %collective-permute-done.20.refs_10_.refs_28_), channel_id=1, source_target_pairs={{0,2},{1,3},{2,0},{3,1},{4,8},{5,9},{6,10},{7,11},{8,4},{9,5},{10,... | collective-permute-start | bytes 393224 | tf_op jit(solution)/shard_map/ppermute | solution.py:149
  29.0 1.0 %collective-permute-done.21.refs_11_.refs_29_ = bf16[64,1024]{1,0:T(8,128)(2,1)S(1)} collective-permute-done((bf16[64,1024]{1,0:T(8,128)(2,1)S(1)}, bf16[64,1024]{1,0:T(8,128)(2,1)S(1)}, u32[]{:S(2)}, u32[]{:S(2)}) %collective-permute-start.21) | collective-permute-done | bytes 131104 | tf_op jit(solution)/shard_map/ppermute | solution.py:149
  30.0 1.8 %collective-permute-done.19.refs_9_.refs_27_ = bf16[64,1024]{1,0:T(8,128)(2,1)S(1)} collective-permute-done((bf16[64,1024]{1,0:T(8,128)(2,1)S(1)}, bf16[64,1024]{1,0:T(8,128)(2,1)S(1)}, u32[]{:S(2)}, u32[]{:S(2)}) %collective-permute-start.19) | collective-permute-done | bytes 131104 | tf_op jit(solution)/shard_map/ppermute | solution.py:149
  31.8 0.8 %collective-permute-start.27 = (bf16[64,1024]{1,0:T(8,128)(2,1)S(1)}, bf16[64,1024]{1,0:T(8,128)(2,1)}, u32[]{:S(2)}, u32[]{:S(2)}) collective-permute-start(bf16[64,1024]{1,0:T(8,128)(2,1)S(1)} %collective-permute-done.19.refs_9_.refs_27_), channel_id=1, source_target_pairs={{0,4},{1,5},{2,6},{3,7},{4,0},{5,1},{6,2},{7,3},{8,12},{9,13},{10,... | collective-permute-start | bytes 393224 | tf_op jit(solution)/shard_map/ppermute | solution.py:149
  32.7 0.5 %collective-permute-start.25 = (bf16[64,1024]{1,0:T(8,128)(2,1)S(1)}, bf16[64,1024]{1,0:T(8,128)(2,1)}, u32[]{:S(2)}, u32[]{:S(2)}) collective-permute-start(bf16[64,1024]{1,0:T(8,128)(2,1)S(1)} %collective-permute-done.21.refs_11_.refs_29_), channel_id=1, source_target_pairs={{0,1},{1,0},{2,3},{3,2},{4,5},{5,4},{6,7},{7,6},{8,9},{9,8},{10,11... | collective-permute-start | bytes 393224 | tf_op jit(solution)/shard_map/ppermute | solution.py:152
  33.2 1.1 %collective-permute-done.26.refs_4_.refs_34_ = bf16[64,1024]{1,0:T(8,128)(2,1)S(1)} collective-permute-done((bf16[64,1024]{1,0:T(8,128)(2,1)S(1)}, bf16[64,1024]{1,0:T(8,128)(2,1)S(1)}, u32[]{:S(2)}, u32[]{:S(2)}) %collective-permute-start.26) | collective-permute-done | bytes 131104 | tf_op jit(solution)/shard_map/ppermute | solution.py:149
  34.3 0.7 %copy-done = bf16[64,1024]{1,0:T(8,128)(2,1)} copy-done((bf16[64,1024]{1,0:T(8,128)(2,1)}, bf16[64,1024]{1,0:T(8,128)(2,1)S(1)}, u32[]{:S(2)}) %copy-start) | copy-done | bytes 131096
  35.0 0.5 %collective-permute-start.28 = (bf16[64,1024]{1,0:T(8,128)(2,1)S(1)}, bf16[64,1024]{1,0:T(8,128)(2,1)}, u32[]{:S(2)}, u32[]{:S(2)}) collective-permute-start(bf16[64,1024]{1,0:T(8,128)(2,1)S(1)} %collective-permute-done.26.refs_4_.refs_34_), channel_id=1, source_target_pairs={{0,1},{1,0},{2,3},{3,2},{4,5},{5,4},{6,7},{7,6},{8,9},{9,8},{10,11... | collective-permute-start | bytes 393224 | tf_op jit(solution)/shard_map/ppermute | solution.py:152
  35.5 1.4 %collective-permute-done.27.refs_5_.refs_35_ = bf16[64,1024]{1,0:T(8,128)(2,1)} collective-permute-done((bf16[64,1024]{1,0:T(8,128)(2,1)S(1)}, bf16[64,1024]{1,0:T(8,128)(2,1)}, u32[]{:S(2)}, u32[]{:S(2)}) %collective-permute-start.27) | collective-permute-done | bytes 131104 | tf_op jit(solution)/shard_map/ppermute | solution.py:149
  36.9 0.7 %shard_map.50 = (f32[128,768]{1,0:T(8,128)S(1)}, f32[128,128]{1,0:T(8,128)S(1)}) custom-call(s32[1]{0:T(128)} %bitcast.me_ref, bf16[128,1024]{1,0:T(8,128)(2,1)S(1)} %get-tuple-element.14.x_ref, s32[1,128]{1,0:T(1,128)S(1)} %get-tuple-element.15.gen_ref, bf16[64,1024]{1,0:T(8,128)(2,1)S(1)} %get-tuple-element.16.refs_0_.refs_6_, ...), custom_call_target="tpu_custom_call" | custom-call | flops 201326592 | tf_op jit(solution)/shard_map/pallas_call | solution.py:197
  37.6 0.0 copy-start.1
  37.6 0.7 %shard_map.51 = (f32[128,768]{1,0:T(8,128)S(1)}, f32[128,128]{1,0:T(8,128)S(1)}) custom-call(s32[1]{0:T(128)} %bitcast.me_ref, bf16[128,1024]{1,0:T(8,128)(2,1)S(1)} %get-tuple-element.14.x_ref, s32[1,128]{1,0:T(1,128)S(1)} %get-tuple-element.15.gen_ref, bf16[64,1024]{1,0:T(8,128)(2,1)S(1)} %collective-permute-done.10.refs_0_.refs_18_, ...), custom_call_target="tpu_custom_call" | custom-call | flops 201326592 | tf_op jit(solution)/shard_map/pallas_call | solution.py:197
  38.3 0.2 copy-done.1
  38.5 1.5 %shard_map.52 = (f32[128,384]{1,0:T(8,128)S(1)}, f32[128,128]{1,0:T(8,128)S(1)}) custom-call(s32[1]{0:T(128)} %bitcast.me_ref, bf16[128,1024]{1,0:T(8,128)(2,1)S(1)} %get-tuple-element.14.x_ref, s32[1,128]{1,0:T(1,128)S(1)} %get-tuple-element.15.gen_ref, bf16[64,1024]{1,0:T(8,128)(2,1)} %collective-permute-done.22.refs_0_.refs_30_, ...), custom_call_target="tpu_custom_call" | custom-call | flops 100663296 | tf_op jit(solution)/shard_map/pallas_call | solution.py:197
  40.0 3.1 %finish.1 = (bf16[128,1024]{1,0:T(8,128)(2,1)}, f32[1,128]{1,0:T(1,128)}) custom-call(s32[1]{0:T(128)} %bitcast.me_ref, bf16[128,1024]{1,0:T(8,128)(2,1)S(1)} %get-tuple-element.14.x_ref, s32[1,128]{1,0:T(1,128)S(1)} %get-tuple-element.15.gen_ref, f32[128,768]{1,0:T(8,128)S(1)} %get-tuple-element.18.refs_0_, f32[128,768]{1,0:T(8,128)S(1)} %get-tuple-element.19.refs_1_, ...), custom_call_target="tpu_custom_call" | custom-call | tf_op jit(solution)/shard_map/finish/pallas_call | solution.py:220
  (27 shorter events, 0.1 us)
Async XLA Ops:
  0.6 0.7 %copy-start.3 = (s32[128]{0:T(128)S(1)}, s32[128]{0:T(128)}, u32[]{:S(2)}) copy-start(s32[128]{0:T(128)} %param.5) | copy-start | bytes 1540
  0.6 0.7 %copy-start.4 = (s32[128]{0:T(128)S(1)}, s32[128]{0:T(128)}, u32[]{:S(2)}) copy-start(s32[128]{0:T(128)} %param.4) | copy-start | bytes 1540
  1.3 0.9 %copy-start.2 = (bf16[128,1024]{1,0:T(8,128)(2,1)S(1)}, bf16[128,1024]{1,0:T(8,128)(2,1)}, u32[]{:S(2)}) copy-start(bf16[128,1024]{1,0:T(8,128)(2,1)} %x_hbm.1) | copy-start | bytes 786436
  2.5 6.4 %collective-permute-start.4 = (bf16[64,1024]{1,0:T(8,128)(2,1)S(1)}, bf16[64,1024]{1,0:T(8,128)(2,1)S(1)}, u32[]{:S(2)}, u32[]{:S(2)}) collective-permute-start(bf16[64,1024]{1,0:T(8,128)(2,1)S(1)} %get-tuple-element.16.refs_0_.refs_6_), channel_id=1, source_target_pairs={{0,1},{1,0},{2,3},{3,2},{4,5},{5,4},{6,7},{7,6},{8,9},{9,8},{10,11... | collective-permute-start | bytes 393224 | tf_op jit(solution)/shard_map/ppermute | solution.py:152
  3.0 7.3 %collective-permute-start.2 = (bf16[64,1024]{1,0:T(8,128)(2,1)S(1)}, bf16[64,1024]{1,0:T(8,128)(2,1)S(1)}, u32[]{:S(2)}, u32[]{:S(2)}) collective-permute-start(bf16[64,1024]{1,0:T(8,128)(2,1)S(1)} %get-tuple-element.16.refs_0_.refs_6_), channel_id=1, source_target_pairs={{0,4},{1,5},{2,6},{3,7},{4,0},{5,1},{6,2},{7,3},{8,12},{9,13},{10,... | collective-permute-start | bytes 393224 | tf_op jit(solution)/shard_map/ppermute | solution.py:149
  5.6 5.8 %collective-permute-start = (bf16[64,1024]{1,0:T(8,128)(2,1)S(1)}, bf16[64,1024]{1,0:T(8,128)(2,1)S(1)}, u32[]{:S(2)}, u32[]{:S(2)}) collective-permute-start(bf16[64,1024]{1,0:T(8,128)(2,1)S(1)} %get-tuple-element.16.refs_0_.refs_6_), channel_id=1, source_target_pairs={{0,2},{1,3},{2,0},{3,1},{4,8},{5,9},{6,10},{7,11},{8,4},{9,5},{10,... | collective-permute-start | bytes 393224 | tf_op jit(solution)/shard_map/ppermute | solution.py:149
  7.2 4.3 %collective-permute-start.5 = (bf16[64,1024]{1,0:T(8,128)(2,1)S(1)}, bf16[64,1024]{1,0:T(8,128)(2,1)S(1)}, u32[]{:S(2)}, u32[]{:S(2)}) collective-permute-start(bf16[64,1024]{1,0:T(8,128)(2,1)S(1)} %get-tuple-element.17.refs_1_.refs_7_), channel_id=1, source_target_pairs={{0,1},{1,0},{2,3},{3,2},{4,5},{5,4},{6,7},{7,6},{8,9},{9,8},{10,11... | collective-permute-start | bytes 393224 | tf_op jit(solution)/shard_map/ppermute | solution.py:152
  7.2 6.5 %collective-permute-start.3 = (bf16[64,1024]{1,0:T(8,128)(2,1)S(1)}, bf16[64,1024]{1,0:T(8,128)(2,1)S(1)}, u32[]{:S(2)}, u32[]{:S(2)}) collective-permute-start(bf16[64,1024]{1,0:T(8,128)(2,1)S(1)} %get-tuple-element.17.refs_1_.refs_7_), channel_id=1, source_target_pairs={{0,4},{1,5},{2,6},{3,7},{4,0},{5,1},{6,2},{7,3},{8,12},{9,13},{10,... | collective-permute-start | bytes 393224 | tf_op jit(solution)/shard_map/ppermute | solution.py:149
  8.8 6.4 %collective-permute-start.1 = (bf16[64,1024]{1,0:T(8,128)(2,1)S(1)}, bf16[64,1024]{1,0:T(8,128)(2,1)S(1)}, u32[]{:S(2)}, u32[]{:S(2)}) collective-permute-start(bf16[64,1024]{1,0:T(8,128)(2,1)S(1)} %get-tuple-element.17.refs_1_.refs_7_), channel_id=1, source_target_pairs={{0,2},{1,3},{2,0},{3,1},{4,8},{5,9},{6,10},{7,11},{8,4},{9,5},{10,... | collective-permute-start | bytes 393224 | tf_op jit(solution)/shard_map/ppermute | solution.py:149
  10.3 7.4 %collective-permute-start.10 = (bf16[64,1024]{1,0:T(8,128)(2,1)S(1)}, bf16[64,1024]{1,0:T(8,128)(2,1)S(1)}, u32[]{:S(2)}, u32[]{:S(2)}) collective-permute-start(bf16[64,1024]{1,0:T(8,128)(2,1)S(1)} %collective-permute-done.2.refs_4_.refs_10_), channel_id=1, source_target_pairs={{0,2},{1,3},{2,0},{3,1},{4,8},{5,9},{6,10},{7,11},{8,4},{9,5},{10,... | collective-permute-start | bytes 393224 | tf_op jit(solution)/shard_map/ppermute | solution.py:149
  11.4 6.3 %collective-permute-start.8 = (bf16[64,1024]{1,0:T(8,128)(2,1)S(1)}, bf16[64,1024]{1,0:T(8,128)(2,1)S(1)}, u32[]{:S(2)}, u32[]{:S(2)}) collective-permute-start(bf16[64,1024]{1,0:T(8,128)(2,1)S(1)} %collective-permute-done.2.refs_4_.refs_10_), channel_id=1, source_target_pairs={{0,1},{1,0},{2,3},{3,2},{4,5},{5,4},{6,7},{7,6},{8,9},{9,8},{10,11... | collective-permute-start | bytes 393224 | tf_op jit(solution)/shard_map/ppermute | solution.py:152
  11.4 6.9 %collective-permute-start.12 = (bf16[64,1024]{1,0:T(8,128)(2,1)S(1)}, bf16[64,1024]{1,0:T(8,128)(2,1)S(1)}, u32[]{:S(2)}, u32[]{:S(2)}) collective-permute-start(bf16[64,1024]{1,0:T(8,128)(2,1)S(1)} %collective-permute-done.refs_2_.refs_8_), channel_id=1, source_target_pairs={{0,4},{1,5},{2,6},{3,7},{4,0},{5,1},{6,2},{7,3},{8,12},{9,13},{10,... | collective-permute-start | bytes 393224 | tf_op jit(solution)/shard_map/ppermute | solution.py:149
  13.7 4.9 %collective-permute-start.6 = (bf16[64,1024]{1,0:T(8,128)(2,1)S(1)}, bf16[64,1024]{1,0:T(8,128)(2,1)S(1)}, u32[]{:S(2)}, u32[]{:S(2)}) collective-permute-start(bf16[64,1024]{1,0:T(8,128)(2,1)S(1)} %collective-permute-done.refs_2_.refs_8_), channel_id=1, source_target_pairs={{0,1},{1,0},{2,3},{3,2},{4,5},{5,4},{6,7},{7,6},{8,9},{9,8},{10,11... | collective-permute-start | bytes 393224 | tf_op jit(solution)/shard_map/ppermute | solution.py:152
  15.2 5.0 %collective-permute-start.11 = (bf16[64,1024]{1,0:T(8,128)(2,1)S(1)}, bf16[64,1024]{1,0:T(8,128)(2,1)S(1)}, u32[]{:S(2)}, u32[]{:S(2)}) collective-permute-start(bf16[64,1024]{1,0:T(8,128)(2,1)S(1)} %collective-permute-done.3.refs_5_.refs_11_), channel_id=1, source_target_pairs={{0,2},{1,3},{2,0},{3,1},{4,8},{5,9},{6,10},{7,11},{8,4},{9,5},{10,... | collective-permute-start | bytes 393224 | tf_op jit(solution)/shard_map/ppermute | solution.py:149
  17.7 2.4 %collective-permute-start.9 = (bf16[64,1024]{1,0:T(8,128)(2,1)S(1)}, bf16[64,1024]{1,0:T(8,128)(2,1)S(1)}, u32[]{:S(2)}, u32[]{:S(2)}) collective-permute-start(bf16[64,1024]{1,0:T(8,128)(2,1)S(1)} %collective-permute-done.3.refs_5_.refs_11_), channel_id=1, source_target_pairs={{0,1},{1,0},{2,3},{3,2},{4,5},{5,4},{6,7},{7,6},{8,9},{9,8},{10,11... | collective-permute-start | bytes 393224 | tf_op jit(solution)/shard_map/ppermute | solution.py:152
  17.7 6.4 %collective-permute-start.13 = (bf16[64,1024]{1,0:T(8,128)(2,1)S(1)}, bf16[64,1024]{1,0:T(8,128)(2,1)S(1)}, u32[]{:S(2)}, u32[]{:S(2)}) collective-permute-start(bf16[64,1024]{1,0:T(8,128)(2,1)S(1)} %collective-permute-done.1.refs_3_.refs_9_), channel_id=1, source_target_pairs={{0,4},{1,5},{2,6},{3,7},{4,0},{5,1},{6,2},{7,3},{8,12},{9,13},{10,... | collective-permute-start | bytes 393224 | tf_op jit(solution)/shard_map/ppermute | solution.py:149
  18.3 5.8 %collective-permute-start.7 = (bf16[64,1024]{1,0:T(8,128)(2,1)S(1)}, bf16[64,1024]{1,0:T(8,128)(2,1)S(1)}, u32[]{:S(2)}, u32[]{:S(2)}) collective-permute-start(bf16[64,1024]{1,0:T(8,128)(2,1)S(1)} %collective-permute-done.1.refs_3_.refs_9_), channel_id=1, source_target_pairs={{0,1},{1,0},{2,3},{3,2},{4,5},{5,4},{6,7},{7,6},{8,9},{9,8},{10,11... | collective-permute-start | bytes 393224 | tf_op jit(solution)/shard_map/ppermute | solution.py:152
  18.6 7.9 %collective-permute-start.20 = (bf16[64,1024]{1,0:T(8,128)(2,1)S(1)}, bf16[64,1024]{1,0:T(8,128)(2,1)S(1)}, u32[]{:S(2)}, u32[]{:S(2)}) collective-permute-start(bf16[64,1024]{1,0:T(8,128)(2,1)S(1)} %collective-permute-done.10.refs_0_.refs_18_), channel_id=1, source_target_pairs={{0,4},{1,5},{2,6},{3,7},{4,0},{5,1},{6,2},{7,3},{8,12},{9,13},{10,... | collective-permute-start | bytes 393224 | tf_op jit(solution)/shard_map/ppermute | solution.py:149
  20.1 7.8 %collective-permute-start.14 = (bf16[64,1024]{1,0:T(8,128)(2,1)S(1)}, bf16[64,1024]{1,0:T(8,128)(2,1)S(1)}, u32[]{:S(2)}, u32[]{:S(2)}) collective-permute-start(bf16[64,1024]{1,0:T(8,128)(2,1)S(1)} %collective-permute-done.10.refs_0_.refs_18_), channel_id=1, source_target_pairs={{0,1},{1,0},{2,3},{3,2},{4,5},{5,4},{6,7},{7,6},{8,9},{9,8},{10,11... | collective-permute-start | bytes 393224 | tf_op jit(solution)/shard_map/ppermute | solution.py:152
  20.2 7.8 %collective-permute-start.18 = (bf16[64,1024]{1,0:T(8,128)(2,1)S(1)}, bf16[64,1024]{1,0:T(8,128)(2,1)S(1)}, u32[]{:S(2)}, u32[]{:S(2)}) collective-permute-start(bf16[64,1024]{1,0:T(8,128)(2,1)S(1)} %collective-permute-done.12.refs_2_.refs_20_), channel_id=1, source_target_pairs={{0,2},{1,3},{2,0},{3,1},{4,8},{5,9},{6,10},{7,11},{8,4},{9,5},{10,... | collective-permute-start | bytes 393224 | tf_op jit(solution)/shard_map/ppermute | solution.py:149
  24.1 4.4 %collective-permute-start.16 = (bf16[64,1024]{1,0:T(8,128)(2,1)S(1)}, bf16[64,1024]{1,0:T(8,128)(2,1)S(1)}, u32[]{:S(2)}, u32[]{:S(2)}) collective-permute-start(bf16[64,1024]{1,0:T(8,128)(2,1)S(1)} %collective-permute-done.12.refs_2_.refs_20_), channel_id=1, source_target_pairs={{0,1},{1,0},{2,3},{3,2},{4,5},{5,4},{6,7},{7,6},{8,9},{9,8},{10,11... | collective-permute-start | bytes 393224 | tf_op jit(solution)/shard_map/ppermute | solution.py:152
  24.1 5.9 %collective-permute-start.21 = (bf16[64,1024]{1,0:T(8,128)(2,1)S(1)}, bf16[64,1024]{1,0:T(8,128)(2,1)S(1)}, u32[]{:S(2)}, u32[]{:S(2)}) collective-permute-start(bf16[64,1024]{1,0:T(8,128)(2,1)S(1)} %collective-permute-done.11.refs_1_.refs_19_), channel_id=1, source_target_pairs={{0,4},{1,5},{2,6},{3,7},{4,0},{5,1},{6,2},{7,3},{8,12},{9,13},{10,... | collective-permute-start | bytes 393224 | tf_op jit(solution)/shard_map/ppermute | solution.py:149
  26.4 5.4 %collective-permute-start.19 = (bf16[64,1024]{1,0:T(8,128)(2,1)S(1)}, bf16[64,1024]{1,0:T(8,128)(2,1)S(1)}, u32[]{:S(2)}, u32[]{:S(2)}) collective-permute-start(bf16[64,1024]{1,0:T(8,128)(2,1)S(1)} %collective-permute-done.13.refs_3_.refs_21_), channel_id=1, source_target_pairs={{0,2},{1,3},{2,0},{3,1},{4,8},{5,9},{6,10},{7,11},{8,4},{9,5},{10,... | collective-permute-start | bytes 393224 | tf_op jit(solution)/shard_map/ppermute | solution.py:149
  28.0 4.7 %collective-permute-start.15 = (bf16[64,1024]{1,0:T(8,128)(2,1)S(1)}, bf16[64,1024]{1,0:T(8,128)(2,1)S(1)}, u32[]{:S(2)}, u32[]{:S(2)}) collective-permute-start(bf16[64,1024]{1,0:T(8,128)(2,1)S(1)} %collective-permute-done.11.refs_1_.refs_19_), channel_id=1, source_target_pairs={{0,1},{1,0},{2,3},{3,2},{4,5},{5,4},{6,7},{7,6},{8,9},{9,8},{10,11... | collective-permute-start | bytes 393224 | tf_op jit(solution)/shard_map/ppermute | solution.py:152
  28.0 4.7 %collective-permute-start.17 = (bf16[64,1024]{1,0:T(8,128)(2,1)S(1)}, bf16[64,1024]{1,0:T(8,128)(2,1)S(1)}, u32[]{:S(2)}, u32[]{:S(2)}) collective-permute-start(bf16[64,1024]{1,0:T(8,128)(2,1)S(1)} %collective-permute-done.13.refs_3_.refs_21_), channel_id=1, source_target_pairs={{0,1},{1,0},{2,3},{3,2},{4,5},{5,4},{6,7},{7,6},{8,9},{9,8},{10,11... | collective-permute-start | bytes 393224 | tf_op jit(solution)/shard_map/ppermute | solution.py:152
  28.5 5.8 %collective-permute-start.26 = (bf16[64,1024]{1,0:T(8,128)(2,1)S(1)}, bf16[64,1024]{1,0:T(8,128)(2,1)S(1)}, u32[]{:S(2)}, u32[]{:S(2)}) collective-permute-start(bf16[64,1024]{1,0:T(8,128)(2,1)S(1)} %collective-permute-done.20.refs_10_.refs_28_), channel_id=1, source_target_pairs={{0,2},{1,3},{2,0},{3,1},{4,8},{5,9},{6,10},{7,11},{8,4},{9,5},{10,... | collective-permute-start | bytes 393224 | tf_op jit(solution)/shard_map/ppermute | solution.py:149
  30.0 4.3 %collective-permute-start.24 = (bf16[64,1024]{1,0:T(8,128)(2,1)S(1)}, bf16[64,1024]{1,0:T(8,128)(2,1)S(1)}, u32[]{:S(2)}, u32[]{:S(2)}) collective-permute-start(bf16[64,1024]{1,0:T(8,128)(2,1)S(1)} %collective-permute-done.20.refs_10_.refs_28_), channel_id=1, source_target_pairs={{0,1},{1,0},{2,3},{3,2},{4,5},{5,4},{6,7},{7,6},{8,9},{9,8},{10,11... | collective-permute-start | bytes 393224 | tf_op jit(solution)/shard_map/ppermute | solution.py:152
  31.8 5.1 %collective-permute-start.27 = (bf16[64,1024]{1,0:T(8,128)(2,1)S(1)}, bf16[64,1024]{1,0:T(8,128)(2,1)}, u32[]{:S(2)}, u32[]{:S(2)}) collective-permute-start(bf16[64,1024]{1,0:T(8,128)(2,1)S(1)} %collective-permute-done.19.refs_9_.refs_27_), channel_id=1, source_target_pairs={{0,4},{1,5},{2,6},{3,7},{4,0},{5,1},{6,2},{7,3},{8,12},{9,13},{10,... | collective-permute-start | bytes 393224 | tf_op jit(solution)/shard_map/ppermute | solution.py:149
  32.7 5.6 %collective-permute-start.22 = (bf16[64,1024]{1,0:T(8,128)(2,1)S(1)}, bf16[64,1024]{1,0:T(8,128)(2,1)}, u32[]{:S(2)}, u32[]{:S(2)}) collective-permute-start(bf16[64,1024]{1,0:T(8,128)(2,1)S(1)} %collective-permute-done.18.refs_8_.refs_26_), channel_id=1, source_target_pairs={{0,1},{1,0},{2,3},{3,2},{4,5},{5,4},{6,7},{7,6},{8,9},{9,8},{10,11... | collective-permute-start | bytes 393224 | tf_op jit(solution)/shard_map/ppermute | solution.py:152
  32.7 5.6 %collective-permute-start.25 = (bf16[64,1024]{1,0:T(8,128)(2,1)S(1)}, bf16[64,1024]{1,0:T(8,128)(2,1)}, u32[]{:S(2)}, u32[]{:S(2)}) collective-permute-start(bf16[64,1024]{1,0:T(8,128)(2,1)S(1)} %collective-permute-done.21.refs_11_.refs_29_), channel_id=1, source_target_pairs={{0,1},{1,0},{2,3},{3,2},{4,5},{5,4},{6,7},{7,6},{8,9},{9,8},{10,11... | collective-permute-start | bytes 393224 | tf_op jit(solution)/shard_map/ppermute | solution.py:152
  34.3 4.0 %collective-permute-start.23 = (bf16[64,1024]{1,0:T(8,128)(2,1)S(1)}, bf16[64,1024]{1,0:T(8,128)(2,1)}, u32[]{:S(2)}, u32[]{:S(2)}) collective-permute-start(bf16[64,1024]{1,0:T(8,128)(2,1)S(1)} %collective-permute-done.19.refs_9_.refs_27_), channel_id=1, source_target_pairs={{0,1},{1,0},{2,3},{3,2},{4,5},{5,4},{6,7},{7,6},{8,9},{9,8},{10,11... | collective-permute-start | bytes 393224 | tf_op jit(solution)/shard_map/ppermute | solution.py:152
  34.3 0.7 %copy-start = (bf16[64,1024]{1,0:T(8,128)(2,1)}, bf16[64,1024]{1,0:T(8,128)(2,1)S(1)}, u32[]{:S(2)}) copy-start(bf16[64,1024]{1,0:T(8,128)(2,1)S(1)} %collective-permute-done.24.refs_2_.refs_32_) | copy-start | bytes 393220
  35.0 5.0 %collective-permute-start.28 = (bf16[64,1024]{1,0:T(8,128)(2,1)S(1)}, bf16[64,1024]{1,0:T(8,128)(2,1)}, u32[]{:S(2)}, u32[]{:S(2)}) collective-permute-start(bf16[64,1024]{1,0:T(8,128)(2,1)S(1)} %collective-permute-done.26.refs_4_.refs_34_), channel_id=1, source_target_pairs={{0,1},{1,0},{2,3},{3,2},{4,5},{5,4},{6,7},{7,6},{8,9},{9,8},{10,11... | collective-permute-start | bytes 393224 | tf_op jit(solution)/shard_map/ppermute | solution.py:152
  36.9 3.1 %collective-permute-start.29 = (bf16[64,1024]{1,0:T(8,128)(2,1)}, bf16[64,1024]{1,0:T(8,128)(2,1)}, u32[]{:S(2)}, u32[]{:S(2)}) collective-permute-start(bf16[64,1024]{1,0:T(8,128)(2,1)} %collective-permute-done.27.refs_5_.refs_35_), channel_id=1, source_target_pairs={{0,1},{1,0},{2,3},{3,2},{4,5},{5,4},{6,7},{7,6},{8,9},{9,8},{10,11... | collective-permute-start | bytes 393224 | tf_op jit(solution)/shard_map/ppermute | solution.py:152
  37.6 0.9 %copy-start.1 = (bf16[64,1024]{1,0:T(8,128)(2,1)S(1)}, bf16[64,1024]{1,0:T(8,128)(2,1)}, u32[]{:S(2)}) copy-start(bf16[64,1024]{1,0:T(8,128)(2,1)} %copy-done) | copy-start | bytes 393220
